TPU v7x, 256 devices: a whole 4x4x8 slice. The times are simulated.
256 devices in a mesh: row: 16 (over x_hi, z), col: 16 (over y, x_lo, core).
Axes of the slice: x: 4 (x_hi: 2, x_lo: 2; x = x_hi * 2 + x_lo), y: 4, z: 8, core: 2. Of those that a mesh axis runs over, the one named last changes fastest.
Arguments:
- objective: float32 [256, 32768], P('row', 'col'), may hold values from -6 to 6
- center: bfloat16 [256, 32768], P('row', 'col'), may hold values from -5 to 5
- radius: bfloat16 [256, 32768], P('row', 'col'), may hold values from 0.049804688 to 1
- lower_gap: bfloat16 [3, 256, 32768], P(None, 'row', 'col'), may hold values from 0.19921875 to 3
- upper_gap: bfloat16 [3, 256, 32768], P(None, 'row', 'col'), may hold values from 0.19921875 to 3
- kernels: float32 [4, 3, 3, 64, 64], replicated, may hold values from -0.25 to 0.25
- biases: float32 [4, 64], replicated, may hold values from -3 to 3
- step_sizes: float32 [3], replicated, may hold values from 0.2 to 1
Outputs:
- bounds: float32 [3], replicated
- final_duals: float32 [3, 256, 32768], P(None, 'row', 'col')
- final_multipliers: float32 [3, 256, 32768], P(None, 'row', 'col')
All inputs are finite; a program needn't handle non-finite values.
Results may differ from a plain program's by a relative error of at most 0.0003.
Values sent between devices are 32-bit elements; how exact they have to be, the bound alone decides.
A program may use at most 128 MiB of HBM per device.

v0:
```python
import jax
import jax.numpy as jnp
from jax import lax
from jax.sharding import PartitionSpec as P

CH = 64
LAYERS = 4
ITERS = 3


TEMP = 0.5
EPS = 1e-06


def extended(cells, sides, width):
    for axis, dim in sides:
        count = lax.axis_size(axis)
        ends = count - 1
        head = lax.slice_in_dim(cells, 0, width, axis=dim)
        tail = lax.slice_in_dim(cells, cells.shape[dim] - width, cells.shape[dim], axis=dim)
        cells = jnp.concatenate(
            [
                lax.ppermute(tail, axis, [(i, (i + 1) % count) for i in range(ends)]),
                cells,
                lax.ppermute(head, axis, [((i + 1) % count, i) for i in range(ends)]),
            ],
            axis=dim,
        )
    return cells


def soft_value(coef, low, high):
    return coef * low - TEMP * jax.nn.softplus(coef * (low - high) / TEMP)


def soft_point(coef, low, high):
    return low + (high - low) * jax.nn.sigmoid(coef * (low - high) / TEMP)


def flipped(kernel):
    return jnp.transpose(kernel[::-1, ::-1], (0, 1, 3, 2))


def conv_valid(padded, kernel):
    out_rows = padded.shape[0] - 2
    out_cols = padded.shape[1] - 2
    in_chan = padded.shape[2]
    result = jnp.zeros((out_rows * out_cols, kernel.shape[3]), jnp.float32)
    for offset_row in range(3):
        for offset_col in range(3):
            window = padded[
                offset_row : offset_row + out_rows, offset_col : offset_col + out_cols
            ].reshape(out_rows * out_cols, in_chan)
            result = result + jnp.dot(
                window,
                kernel[offset_row, offset_col],
                precision=lax.Precision.HIGHEST,
                preferred_element_type=jnp.float32,
            )
    return result.reshape(out_rows, out_cols, kernel.shape[3])


def shards(objective, center, radius, lower_gap, upper_gap, kernels, biases, step_sizes):
    depth = LAYERS - 1
    tile_rows = objective.shape[0]
    tile_cols = objective.shape[1] // CH

    def cube(plane):
        return plane.reshape(plane.shape[:-1] + (tile_cols, CH))

    target = cube(objective)
    target_rim = extended(target, (("row", 0), ("col", 1)), 1)
    target_back = conv_valid(target_rim, flipped(kernels[LAYERS - 1]))
    fixed_part = jnp.sum(target * biases[LAYERS - 1])
    middle = cube(center.astype(jnp.float32))
    half = cube(radius.astype(jnp.float32))
    below = cube(lower_gap.astype(jnp.float32))
    above = cube(upper_gap.astype(jnp.float32))
    zero_map = jnp.zeros_like(middle)
    lows = [middle - half] + [zero_map] * depth
    highs = [middle + half] + [above[j] for j in range(depth)]
    duals = jnp.zeros((depth, tile_rows, tile_cols, CH), jnp.float32)
    multipliers = jnp.zeros_like(duals)
    total_cells = tile_rows * tile_cols * CH * lax.axis_size("row") * lax.axis_size("col")
    bounds = []
    for step in range(ITERS):
        coefs = []
        dual_rim = extended(duals, (("row", 1), ("col", 2)), 1)
        for layer in range(depth):
            coef = -conv_valid(dual_rim[layer], flipped(kernels[layer]))
            if layer > 0:
                coef = coef + multipliers[layer - 1]
            coefs.append(coef)
        points = [soft_point(coefs[layer], lows[layer], highs[layer]) for layer in range(depth)]
        primal = extended(jnp.stack(points), (("row", 1), ("col", 2)), 1)
        input_rims = [primal[layer] for layer in range(depth)]
        coefs.append(target_back + multipliers[depth - 1])
        points.append(soft_point(coefs[depth], lows[depth], highs[depth]))
        value = fixed_part
        for layer in range(LAYERS):
            value = value + jnp.sum(soft_value(coefs[layer], lows[layer], highs[layer]))
        slope_duals = []
        slope_mults = []
        squares = jnp.zeros((), jnp.float32)
        for j in range(depth):
            pos_coef = duals[j] - multipliers[j]
            neg_coef = -duals[j]
            value = value + jnp.sum(soft_value(pos_coef, zero_map, above[j]))
            value = value + jnp.sum(soft_value(neg_coef, zero_map, below[j]))
            value = value - jnp.sum(duals[j] * biases[j])
            positive = soft_point(pos_coef, zero_map, above[j])
            negative = soft_point(neg_coef, zero_map, below[j])
            slope_dual = positive - negative - conv_valid(input_rims[j], kernels[j]) - biases[j]
            slope_mult = points[j + 1] - positive
            squares = squares + jnp.sum(slope_dual * slope_dual) + jnp.sum(slope_mult * slope_mult)
            slope_duals.append(slope_dual)
            slope_mults.append(slope_mult)
        total_squares, total_value = lax.psum((squares, value), ("row", "col"))
        bounds.append(total_value / total_cells)
        scale = step_sizes[step] / jnp.sqrt(total_squares / (2 * depth * total_cells) + EPS)
        duals = duals + scale * jnp.stack(slope_duals)
        multipliers = multipliers + scale * jnp.stack(slope_mults)
    bound_array = jnp.stack(bounds)
    final_duals = duals.reshape(depth, tile_rows, tile_cols * CH)
    final_multipliers = multipliers.reshape(depth, tile_rows, tile_cols * CH)
    return (bound_array, final_duals, final_multipliers)


def solution(mesh):
    placed = (
        P("row", "col"),
        P("row", "col"),
        P("row", "col"),
        P(None, "row", "col"),
        P(None, "row", "col"),
        P(),
        P(),
        P(),
    )
    return jax.shard_map(
        shards,
        mesh=mesh,
        in_specs=placed,
        out_specs=(P(), P(None, "row", "col"), P(None, "row", "col")),
        check_vma=False,
    )
```

profile of v0, /device:TPU:1, one launch (start us, length us, event | category | flops | bytes accessed | tf_op | source)
XLA Modules:
  0.0 666.4 jit_solution(15798143236063260089)
XLA Ops:
  1.3 5.0 collective-permute-start
  8.5 4.0 collective-permute-start.4
  30.5 1.7 copy.172
  32.3 1.7 copy.177
  40.0 4.5 collective-permute-start.6
  44.5 1.9 collective-permute-start.7
  54.1 2.1 collective-permute-start.2
  56.2 2.4 collective-permute-start.3
  59.7 2.3 collective-permute-done.3
  68.6 1.7 copy.179
  82.6 1.8 fusion.139
  86.0 4.3 collective-permute-start.8
  93.7 1.8 neg.745
  96.6 3.1 collective-permute-start.10
  99.7 2.1 collective-permute-start.11
  101.8 2.3 multiply_reduce_fusion.14
  104.1 1.7 neg.740
  123.5 1.8 multiply_reduce_fusion.13
  126.5 2.6 subtract_subtract_fusion.11
  132.9 88.6 %psum.43 = f32[]{:T(128)} all-reduce(f32[]{:T(128)S(6)} %add.1337), channel_id=1, replica_groups=mesh['row'=16,'col'=16] {'row','col'}, use_global_device_ids=true, to_apply=%region_21.22 | all-reduce | flops 1 | bytes 8 | tf_op jit(solution)/shard_map/psum | solution.py:118
  224.9 2.1 collective-permute-start.12
  229.9 1.9 collective-permute-done.13
  231.9 3.4 collective-permute-start.14
  235.3 2.6 collective-permute-start.15
  238.0 2.5 collective-permute-done.15
  246.3 1.8 copy.202
  260.6 2.4 fusion.140
  263.7 2.3 collective-permute-start.16
  268.5 2.6 collective-permute-done.17
  272.6 3.3 collective-permute-start.18
  275.9 2.1 collective-permute-start.19
  301.6 1.7 copy.216
  309.0 2.7 multiply_subtract_fusion.1
  311.7 1.8 squeeze.642
  323.6 1.7 multiply_reduce_fusion.11
  325.3 2.3 multiply_reduce_fusion.6
  337.7 83.4 %psum.45 = f32[]{:T(128)} all-reduce(f32[]{:T(128)S(6)} %add.1442), channel_id=1, replica_groups=mesh['row'=16,'col'=16] {'row','col'}, use_global_device_ids=true, to_apply=%region_42.43 | all-reduce | flops 1 | bytes 8 | tf_op jit(solution)/shard_map/psum | solution.py:118
  425.6 2.2 collective-permute-start.20
  432.0 1.8 sub.1031
  433.8 1.8 sub.1036
  435.6 1.7 sub.1042
  438.9 1.8 sub.1040
  443.1 3.1 collective-permute-start.22
  446.2 1.9 collective-permute-start.23
  449.3 2.1 collective-permute-done.23
  457.0 2.0 fusion.77
  459.0 1.7 copy.230
  460.7 2.0 multiply_add_fusion
  473.9 1.7 copy.221
  475.6 2.5 fusion.142
  478.9 4.9 collective-permute-start.24
  485.3 2.1 fusion.69
  488.1 1.8 stack.110
  491.6 1.7 stack.111
  493.4 1.8 pad_maximum_fusion.23
  495.2 2.2 collective-permute-start.26
  497.4 2.9 collective-permute-start.27
  500.3 4.4 fusion.41
  504.6 1.8 neg.841
  508.1 1.8 copy.234
  509.9 1.8 squeeze.655
  537.8 2.5 multiply_subtract_fusion
  551.1 2.2 multiply_reduce_fusion
  578.2 81.8 %all-reduce = (f32[]{:T(128)}, f32[]{:T(128)}, f32[]{:T(128)}, f32[]{:T(128)}) all-reduce(f32[]{:T(128)S(6)} %sub.1093, f32[]{:T(128)S(6)} %sub.1044, f32[]{:T(128)S(6)} %sub.986, f32[]{:T(128)S(6)} %add.1554), channel_id=1, replica_groups=mesh['row'=16,'col'=16] {'row','col'}, use_global_device_ids=true, to_apply=%region_56.57 | all-reduce | flops 4 | bytes 32 | tf_op jit(solution)/shard_map/psum | solution.py:118
  (749 shorter events, 220.8 us)
Async XLA Ops:
  1.3 51.9 %collective-permute-start = (f32[3,1,32,64]{3,2,1,0:T(8,128)}, f32[3,1,32,64]{3,2,1,0:T(8,128)}, u32[]{:S(2)}, u32[]{:S(2)}) collective-permute-start(f32[3,1,32,64]{3,2,1,0:T(8,128)} %broadcast.870), channel_id=1, source_target_pairs={{0,16},{16,32},{32,48},{48,64},{64,80},{80,96},{96,112},{112,128},... | collective-permute-start | bytes 73736 | tf_op jit(solution)/shard_map/ppermute | solution.py:23
  6.2 47.0 %collective-permute-start.1 = (f32[3,1,32,64]{3,2,1,0:T(8,128)}, f32[3,1,32,64]{3,2,1,0:T(8,128)}, u32[]{:S(2)}, u32[]{:S(2)}) collective-permute-start(f32[3,1,32,64]{3,2,1,0:T(8,128)} %broadcast.870), channel_id=1, source_target_pairs={{16,0},{32,16},{48,32},{64,48},{80,64},{96,80},{112,96},{128,112},... | collective-permute-start | bytes 73736 | tf_op jit(solution)/shard_map/ppermute | solution.py:25
  8.5 30.2 %collective-permute-start.4 = (f32[1,32,64]{2,1,0:T(8,128)S(1)}, f32[1,32,64]{2,1,0:T(8,128)S(1)}, u32[]{:S(2)}, u32[]{:S(2)}) collective-permute-start(f32[1,32,64]{2,1,0:T(8,128)S(1)} %slice.1193), channel_id=1, source_target_pairs={{0,16},{16,32},{32,48},{48,64},{64,80},{80,96},{96,112},{112,128},... | collective-permute-start | bytes 24584 | tf_op jit(solution)/shard_map/ppermute | solution.py:23
  13.2 25.5 %collective-permute-start.5 = (f32[1,32,64]{2,1,0:T(8,128)}, f32[1,32,64]{2,1,0:T(8,128)S(1)}, u32[]{:S(2)}, u32[]{:S(2)}) collective-permute-start(f32[1,32,64]{2,1,0:T(8,128)} %slice.1195), channel_id=1, source_target_pairs={{16,0},{32,16},{48,32},{64,48},{80,64},{96,80},{112,96},{128,112},... | collective-permute-start | bytes 24584 | tf_op jit(solution)/shard_map/ppermute | solution.py:25
  15.9 94.6 %copy-start.7 = (f32[3,3,64,64]{3,2,1,0:T(8,128)}, f32[3,3,64,64]{3,2,1,0:T(8,128)S(1)}, u32[]{:S(2)}) copy-start(f32[3,3,64,64]{3,2,1,0:T(8,128)S(1)} %get-tuple-element.93) | copy-start | bytes 442372
  15.9 101.8 %copy-start.10 = (f32[3,3,64,64]{3,2,1,0:T(8,128)}, f32[3,3,64,64]{3,2,1,0:T(8,128)S(1)}, u32[]{:S(2)}) copy-start(f32[3,3,64,64]{3,2,1,0:T(8,128)S(1)} %get-tuple-element.92) | copy-start | bytes 442372
  16.0 107.5 %copy-start.4 = (f32[3,3,64,64]{3,2,1,0:T(8,128)}, f32[3,3,64,64]{3,2,1,0:T(8,128)S(1)}, u32[]{:S(2)}) copy-start(f32[3,3,64,64]{3,2,1,0:T(8,128)S(1)} %get-tuple-element.94) | copy-start | bytes 442372
  18.8 204.1 %copy-start.180 = (f32[64]{0:T(128)}, f32[64]{0:T(128)S(1)}, u32[]{:S(2)}) copy-start(f32[64]{0:T(128)S(1)} %get-tuple-element.365) | copy-start | bytes 772
  18.8 205.3 %copy-start.178 = (f32[64]{0:T(128)}, f32[64]{0:T(128)S(1)}, u32[]{:S(2)}) copy-start(f32[64]{0:T(128)S(1)} %get-tuple-element.367) | copy-start | bytes 772
  18.8 205.3 %copy-start.182 = (f32[64]{0:T(128)}, f32[64]{0:T(128)S(1)}, u32[]{:S(2)}) copy-start(f32[64]{0:T(128)S(1)} %get-tuple-element.368) | copy-start | bytes 772
  19.5 18.1 %copy-start.95 = (f32[1,16,2048]{2,1,0:T(8,128)}, f32[1,16,2048]{2,1,0:T(8,128)S(1)}, u32[]{:S(2)}) copy-start(f32[1,16,2048]{2,1,0:T(8,128)S(1)} %get-tuple-element.356) | copy-start | bytes 393220
  28.0 196.1 %copy-start.29 = (f32[1,16,32,64]{3,2,1,0:T(8,128)}, f32[1,16,32,64]{3,2,1,0:T(8,128)S(1)}, u32[]{:S(2)}) copy-start(f32[1,16,32,64]{3,2,1,0:T(8,128)S(1)} %squeeze.619) | copy-start | bytes 393220
  29.7 54.7 %copy-start.32 = (f32[1,16,32,64]{3,2,1,0:T(8,128)}, f32[1,16,32,64]{3,2,1,0:T(8,128)S(1)}, u32[]{:S(2)}) copy-start(f32[1,16,32,64]{3,2,1,0:T(8,128)S(1)} %sub.989) | copy-start | bytes 393220
  37.5 85.9 %copy-start.73 = (f32[512,64]{0,1:T(8,128)}, f32[512,64]{0,1:T(8,128)S(1)}, u32[]{:S(2)}) copy-start(f32[512,64]{0,1:T(8,128)S(1)} %copy.174) | copy-start | bytes 393220
  40.0 8.0 %collective-permute-start.6 = (f32[18,1,64]{2,1,0:T(1,128)S(1)}, f32[18,1,64]{2,1,0:T(1,128)S(1)}, u32[]{:S(2)}, u32[]{:S(2)}) collective-permute-start(f32[18,1,64]{2,1,0:T(1,128)S(1)} %get-tuple-element.347), channel_id=1, source_target_pairs={{0,1},{1,2},{2,3},{3,4},{4,5},{5,6},{6,7},{7,8},{8,9},{9,10},{10,1... | collective-permute-start | bytes 13832 | tf_op jit(solution)/shard_map/ppermute | solution.py:23
  44.5 5.0 collective-permute-start.7
  54.1 5.6 collective-permute-start.2
  56.2 5.8 collective-permute-start.3
  86.0 9.5 %collective-permute-start.8 = (f32[3,1,32,64]{3,2,1,0:T(8,128)}, f32[3,1,32,64]{3,2,1,0:T(8,128)S(1)}, u32[]{:S(2)}, u32[]{:S(2)}) collective-permute-start(f32[3,1,32,64]{3,2,1,0:T(8,128)} %get-tuple-element.160), channel_id=1, source_target_pairs={{0,16},{16,32},{32,48},{48,64},{64,80},{80,96},{96,112},{112,128},... | collective-permute-start | bytes 73736 | tf_op jit(solution)/shard_map/ppermute | solution.py:23
  90.3 5.7 collective-permute-start.9
  93.7 32.8 %copy-start.67 = (f32[1,16,2048]{2,1,0:T(8,128)}, f32[1,16,2048]{2,1,0:T(8,128)S(1)}, u32[]{:S(2)}) copy-start(f32[1,16,2048]{2,1,0:T(8,128)S(1)} %reshape.1670) | copy-start | bytes 393220
  96.6 9.2 %collective-permute-start.10 = (f32[3,18,1,64]{3,2,1,0:T(1,128)}, f32[3,18,1,64]{3,2,1,0:T(1,128)S(1)}, u32[]{:S(2)}, u32[]{:S(2)}) collective-permute-start(f32[3,18,1,64]{3,2,1,0:T(1,128)} %get-tuple-element.121), channel_id=1, source_target_pairs={{0,1},{1,2},{2,3},{3,4},{4,5},{5,6},{6,7},{7,8},{8,9},{9,10},{10,1... | collective-permute-start | bytes 41480 | tf_op jit(solution)/shard_map/ppermute | solution.py:23
  99.7 6.2 collective-permute-start.11
  126.5 96.4 %copy-start.39 = (f32[1,16,32,64]{3,2,1,0:T(8,128)S(1)}, f32[1,16,32,64]{3,2,1,0:T(8,128)}, u32[]{:S(2)}) copy-start(f32[1,16,32,64]{3,2,1,0:T(8,128)} %squeeze.618) | copy-start | bytes 393220
  129.1 95.0 %copy-start.34 = (f32[1,16,32,64]{3,2,1,0:T(8,128)S(1)}, f32[1,16,32,64]{3,2,1,0:T(8,128)}, u32[]{:S(2)}) copy-start(f32[1,16,32,64]{3,2,1,0:T(8,128)} %squeeze.620) | copy-start | bytes 393220
  132.9 91.6 %copy-start.37 = (f32[1,16,32,64]{3,2,1,0:T(8,128)}, f32[1,16,32,64]{3,2,1,0:T(8,128)S(1)}, u32[]{:S(2)}) copy-start(f32[1,16,32,64]{3,2,1,0:T(8,128)S(1)} %squeeze.621) | copy-start | bytes 393220
  224.5 13.4 %copy-start.46 = (f32[1,16,32,64]{3,2,1,0:T(8,128)}, f32[1,16,32,64]{3,2,1,0:T(8,128)S(1)}, u32[]{:S(2)}) copy-start(f32[1,16,32,64]{3,2,1,0:T(8,128)S(1)} %get-tuple-element.349) | copy-start | bytes 393220
  224.9 13.0 %copy-start.56 = (f32[1,16,32,64]{3,2,1,0:T(8,128)S(1)}, f32[1,16,32,64]{3,2,1,0:T(8,128)}, u32[]{:S(2)}) copy-start(f32[1,16,32,64]{3,2,1,0:T(8,128)} %get-tuple-element.162) | copy-start | bytes 393220
  224.9 13.0 %copy-start.58 = (f32[1,16,32,64]{3,2,1,0:T(8,128)S(1)}, f32[1,16,32,64]{3,2,1,0:T(8,128)}, u32[]{:S(2)}) copy-start(f32[1,16,32,64]{3,2,1,0:T(8,128)} %get-tuple-element.164) | copy-start | bytes 393220
  224.9 5.0 collective-permute-start.12
  227.0 4.8 collective-permute-start.13
  231.9 6.1 collective-permute-start.14
  235.3 5.2 collective-permute-start.15
  238.0 71.0 %copy-start = (f32[3,16,32,64]{3,2,1,0:T(8,128)}, f32[3,16,32,64]{3,2,1,0:T(8,128)S(1)}, u32[]{:S(2)}) copy-start(f32[3,16,32,64]{3,2,1,0:T(8,128)S(1)} %maximum_multiply_fusion.1) | copy-start | bytes 1179652
  263.7 4.8 collective-permute-start.16
  266.0 5.2 collective-permute-start.17
  272.6 22.4 %collective-permute-start.18 = (f32[3,18,1,64]{3,2,1,0:T(1,128)}, f32[3,18,1,64]{3,2,1,0:T(1,128)}, u32[]{:S(2)}, u32[]{:S(2)}) collective-permute-start(f32[3,18,1,64]{3,2,1,0:T(1,128)} %get-tuple-element.117), channel_id=1, source_target_pairs={{0,1},{1,2},{2,3},{3,4},{4,5},{5,6},{6,7},{7,8},{8,9},{9,10},{10,1... | collective-permute-start | bytes 41480 | tf_op jit(solution)/shard_map/ppermute | solution.py:23
  275.9 19.1 %collective-permute-start.19 = (f32[3,18,1,64]{3,2,1,0:T(1,128)}, f32[3,18,1,64]{3,2,1,0:T(1,128)}, u32[]{:S(2)}, u32[]{:S(2)}) collective-permute-start(f32[3,18,1,64]{3,2,1,0:T(1,128)} %get-tuple-element.118), channel_id=1, source_target_pairs={{1,0},{2,1},{3,2},{4,3},{5,4},{6,5},{7,6},{8,7},{9,8},{10,9},{11,1... | collective-permute-start | bytes 41480 | tf_op jit(solution)/shard_map/ppermute | solution.py:25
  333.1 88.9 %copy-start.30 = (f32[1,16,32,64]{3,2,1,0:T(8,128)S(1)}, f32[1,16,32,64]{3,2,1,0:T(8,128)}, u32[]{:S(2)}) copy-start(f32[1,16,32,64]{3,2,1,0:T(8,128)} %copy-done.29) | copy-start | bytes 393220
  333.1 88.9 %copy-start.55 = (f32[1,16,32,64]{3,2,1,0:T(8,128)S(1)}, f32[1,16,32,64]{3,2,1,0:T(8,128)}, u32[]{:S(2)}) copy-start(f32[1,16,32,64]{3,2,1,0:T(8,128)} %get-tuple-element.89) | copy-start | bytes 393220
  334.3 89.2 %copy-start.49 = (f32[1,16,32,64]{3,2,1,0:T(8,128)S(1)}, f32[1,16,32,64]{3,2,1,0:T(8,128)}, u32[]{:S(2)}) copy-start(f32[1,16,32,64]{3,2,1,0:T(8,128)} %copy-done.48) | copy-start | bytes 393220
  334.3 89.2 %copy-start.51 = (f32[1,16,32,64]{3,2,1,0:T(8,128)S(1)}, f32[1,16,32,64]{3,2,1,0:T(8,128)}, u32[]{:S(2)}) copy-start(f32[1,16,32,64]{3,2,1,0:T(8,128)} %copy-done.50) | copy-start | bytes 393220
  425.6 16.6 %collective-permute-start.20 = (f32[3,1,32,64]{3,2,1,0:T(8,128)}, f32[3,1,32,64]{3,2,1,0:T(8,128)}, u32[]{:S(2)}, u32[]{:S(2)}) collective-permute-start(f32[3,1,32,64]{3,2,1,0:T(8,128)} %get-tuple-element.150), channel_id=1, source_target_pairs={{0,16},{16,32},{32,48},{48,64},{64,80},{80,96},{96,112},{112,128},... | collective-permute-start | bytes 73736 | tf_op jit(solution)/shard_map/ppermute | solution.py:23
  427.8 14.4 %collective-permute-start.21 = (f32[3,1,32,64]{3,2,1,0:T(8,128)}, f32[3,1,32,64]{3,2,1,0:T(8,128)}, u32[]{:S(2)}, u32[]{:S(2)}) collective-permute-start(f32[3,1,32,64]{3,2,1,0:T(8,128)} %get-tuple-element.151), channel_id=1, source_target_pairs={{16,0},{32,16},{48,32},{64,48},{80,64},{96,80},{112,96},{128,112},... | collective-permute-start | bytes 73736 | tf_op jit(solution)/shard_map/ppermute | solution.py:25
  443.1 6.1 collective-permute-start.22
  446.2 5.2 collective-permute-start.23
  478.9 14.4 %collective-permute-start.24 = (f32[3,1,32,64]{3,2,1,0:T(8,128)}, f32[3,1,32,64]{3,2,1,0:T(8,128)}, u32[]{:S(2)}, u32[]{:S(2)}) collective-permute-start(f32[3,1,32,64]{3,2,1,0:T(8,128)} %get-tuple-element.143), channel_id=1, source_target_pairs={{0,16},{16,32},{32,48},{48,64},{64,80},{80,96},{96,112},{112,128},... | collective-permute-start | bytes 73736 | tf_op jit(solution)/shard_map/ppermute | solution.py:23
  483.8 9.5 %collective-permute-start.25 = (f32[3,1,32,64]{3,2,1,0:T(8,128)}, f32[3,1,32,64]{3,2,1,0:T(8,128)}, u32[]{:S(2)}, u32[]{:S(2)}) collective-permute-start(f32[3,1,32,64]{3,2,1,0:T(8,128)} %get-tuple-element.144), channel_id=1, source_target_pairs={{16,0},{32,16},{48,32},{64,48},{80,64},{96,80},{112,96},{128,112},... | collective-permute-start | bytes 73736 | tf_op jit(solution)/shard_map/ppermute | solution.py:25
  495.2 27.6 %collective-permute-start.26 = (f32[3,18,1,64]{3,2,1,0:T(1,128)}, f32[3,18,1,64]{3,2,1,0:T(1,128)}, u32[]{:S(2)}, u32[]{:S(2)}) collective-permute-start(f32[3,18,1,64]{3,2,1,0:T(1,128)} %get-tuple-element.113), channel_id=1, source_target_pairs={{0,1},{1,2},{2,3},{3,4},{4,5},{5,6},{6,7},{7,8},{8,9},{9,10},{10,1... | collective-permute-start | bytes 41480 | tf_op jit(solution)/shard_map/ppermute | solution.py:23
  497.4 25.5 %collective-permute-start.27 = (f32[3,18,1,64]{3,2,1,0:T(1,128)}, f32[3,18,1,64]{3,2,1,0:T(1,128)}, u32[]{:S(2)}, u32[]{:S(2)}) collective-permute-start(f32[3,18,1,64]{3,2,1,0:T(1,128)} %get-tuple-element.114), channel_id=1, source_target_pairs={{1,0},{2,1},{3,2},{4,3},{5,4},{6,5},{7,6},{8,7},{9,8},{10,9},{11,1... | collective-permute-start | bytes 41480 | tf_op jit(solution)/shard_map/ppermute | solution.py:25
  509.9 12.9 %copy-start.23 = (f32[1,16,32,64]{3,2,1,0:T(8,128)S(1)}, f32[1,16,32,64]{3,2,1,0:T(8,128)}, u32[]{:S(2)}) copy-start(f32[1,16,32,64]{3,2,1,0:T(8,128)} %multiply_add_fusion) | copy-start | bytes 393220
  509.9 13.0 %copy-start.25 = (f32[1,16,32,64]{3,2,1,0:T(8,128)S(1)}, f32[1,16,32,64]{3,2,1,0:T(8,128)}, u32[]{:S(2)}) copy-start(f32[1,16,32,64]{3,2,1,0:T(8,128)} %copy-done.24) | copy-start | bytes 393220
  509.9 13.0 %copy-start.27 = (f32[1,16,32,64]{3,2,1,0:T(8,128)S(1)}, f32[1,16,32,64]{3,2,1,0:T(8,128)}, u32[]{:S(2)}) copy-start(f32[1,16,32,64]{3,2,1,0:T(8,128)} %copy-done.26) | copy-start | bytes 393220
  551.1 27.0 %copy-start.102 = (f32[1,16,32,64]{3,2,1,0:T(8,128)S(1)}, f32[1,16,32,64]{3,2,1,0:T(8,128)}, u32[]{:S(2)}) copy-start(f32[1,16,32,64]{3,2,1,0:T(8,128)} %get-tuple-element.85) | copy-start | bytes 393220
  553.3 107.4 %copy-start.126 = (f32[1,16,32,64]{3,2,1,0:T(8,128)S(1)}, f32[1,16,32,64]{3,2,1,0:T(8,128)}, u32[]{:S(2)}) copy-start(f32[1,16,32,64]{3,2,1,0:T(8,128)} %get-tuple-element.81) | copy-start | bytes 393220
  555.9 105.1 %copy-start.125 = (f32[1,16,32,64]{3,2,1,0:T(8,128)S(1)}, f32[1,16,32,64]{3,2,1,0:T(8,128)}, u32[]{:S(2)}) copy-start(f32[1,16,32,64]{3,2,1,0:T(8,128)} %get-tuple-element.127) | copy-start | bytes 393220
  555.9 105.3 %copy-start.124 = (f32[1,16,32,64]{3,2,1,0:T(8,128)S(1)}, f32[1,16,32,64]{3,2,1,0:T(8,128)}, u32[]{:S(2)}) copy-start(f32[1,16,32,64]{3,2,1,0:T(8,128)} %get-tuple-element.82) | copy-start | bytes 393220
  556.9 107.6 %copy-start.135 = (f32[1,16,2048]{2,1,0:T(8,128)S(1)}, f32[1,16,2048]{2,1,0:T(8,128)}, u32[]{:S(2)}) copy-start(f32[1,16,2048]{2,1,0:T(8,128)} %get-tuple-element.170) | copy-start | bytes 393220
  556.9 107.6 %copy-start.136 = (f32[1,16,2048]{2,1,0:T(8,128)S(1)}, f32[1,16,2048]{2,1,0:T(8,128)}, u32[]{:S(2)}) copy-start(f32[1,16,2048]{2,1,0:T(8,128)} %get-tuple-element.172) | copy-start | bytes 393220
  556.9 107.6 %copy-start.139 = (f32[1,16,2048]{2,1,0:T(8,128)S(1)}, f32[1,16,2048]{2,1,0:T(8,128)}, u32[]{:S(2)}) copy-start(f32[1,16,2048]{2,1,0:T(8,128)} %stack.119) | copy-start | bytes 393220
  556.9 107.6 %copy-start.140 = (f32[1,16,2048]{2,1,0:T(8,128)S(1)}, f32[1,16,2048]{2,1,0:T(8,128)}, u32[]{:S(2)}) copy-start(f32[1,16,2048]{2,1,0:T(8,128)} %stack.120) | copy-start | bytes 393220
  556.9 107.6 %copy-start.147 = (f32[1,16,2048]{2,1,0:T(8,128)S(1)}, f32[1,16,2048]{2,1,0:T(8,128)}, u32[]{:S(2)}) copy-start(f32[1,16,2048]{2,1,0:T(8,128)} %stack.121) | copy-start | bytes 393220
  556.9 107.6 %copy-start.148 = (f32[1,16,2048]{2,1,0:T(8,128)S(1)}, f32[1,16,2048]{2,1,0:T(8,128)}, u32[]{:S(2)}) copy-start(f32[1,16,2048]{2,1,0:T(8,128)} %stack.123) | copy-start | bytes 393220
  556.9 107.6 %copy-start.153 = (f32[1,16,2048]{2,1,0:T(8,128)S(1)}, f32[1,16,2048]{2,1,0:T(8,128)}, u32[]{:S(2)}) copy-start(f32[1,16,2048]{2,1,0:T(8,128)} %get-tuple-element.75) | copy-start | bytes 393220
  (154 other events, 550.2 us)
where the time goes:
time: 675 us; the launch traced here: 666 us
  blocking collectives  254 us (38%)
  local copies, waits for them, and re-layouts  125 us (19%)
  matrix products  87.9 us (13%)
  starting transfers between devices  71.9 us (11%)
  other arithmetic  66.3 us (10%)
  between operations  47.8 us (7%)
  waiting for transfers between devices  13.5 us (2%)
    psum x3, blocking collectives, shards(): total_squares, total_value = lax.psum((squares, value), ('row', 'col'))  254 us
    dot_general x171, matrix products, conv_valid(): jnp.dot(window, kernel[offset_row, offset_col], precision=lax.Precision.H...  87.9 us
    ppermute x14, starting transfers between devices, extended(): lax.ppermute(tail, axis, [(i, (i + 1) % count) for i in range(ends)])  46.3 us
    ppermute x14, starting transfers between devices, extended(): lax.ppermute(head, axis, [((i + 1) % count, i) for i in range(ends)])  25.5 us
    neg x15, local copies, waits for them, and re-layouts, shards(): coef = -conv_valid(dual_rim[layer], flipped(kernels[layer]))  21.6 us
  transfers between devices with their start and end apart: 28, of which 7 were waited for; matrix products, arithmetic and copies ran while one was open for 15% of the time, Pallas kernels for 0%

commit v1 on v0

v1 whole, which is shorter than its diff:
```python
import jax
import jax.numpy as jnp
from jax import lax
from jax.experimental import pallas as pl
from jax.experimental.pallas import tpu as pltpu
from jax.sharding import PartitionSpec as P

CH = 64
LAYERS = 4
ITERS = 3
DEPTH = LAYERS - 1
EPS = 1e-06
MESH = pl.DeviceIdType.MESH
F32 = jnp.float32
BF16 = jnp.bfloat16

ROWS = 16
PAIRS = 16
EXT = 24
EPAIRS = 18
WIDE = 32
PLANES = 8
MID, HALF, H1, H2, OBJ, H3, Q1, Q2, Q3 = range(9)
UP, DOWN, LEFT, RIGHT = range(4)
SIDES = ((-1, 0), (1, 0), (0, -1), (0, 1), (-1, -1), (-1, 1), (1, -1), (1, 1))


def at(start, size):
    return pl.ds(pl.multiple_of(start, 8), size)


def inner(which, pair):
    return at((which * PAIRS + pair) * ROWS, ROWS)


def ext(which, pair):
    return at((which * EPAIRS + pair) * EXT, EXT)


def ext_inner(which, pair):
    return pl.ds((which * EPAIRS + pair + 1) * EXT + 1, ROWS)


def softplus(z):
    return jnp.maximum(z, 0.0) + jnp.log1p(jnp.exp(-jnp.abs(z)))


def split(v):
    hi = v.astype(BF16)
    return hi, (v - hi.astype(F32)).astype(BF16)


def body(total_cells, n_row, n_col, obj_h, cen_h, rad_h, low_h, upp_h, ker_h, bia_h, steps,
         bounds_ref, lam_out, mu_out,
         obj_v, cen_v, rad_v, low_v, upp_v, ker_v, bia_v,
         base, wide_in, lam, mu, lam_x, mu_x, dl, dmu, dmu_x, trans, upd, g_x, x_x, p_x, pn, tb, conv_out,
         d_w, y_s, lhs_i, lhs_x, wts,
         rows_s0, cols_s0, diag_s0, rows_r0, cols_r0, diag_r0,
         rows_s, cols_s, diag_s, rows_r, cols_r, diag_r,
         pay_a, buf_a, pay_b, buf_b,
         load_sem, halo_send, halo_recv, a_send, a_recv, b_send, b_recv):
    row = lax.axis_index("row")
    col = lax.axis_index("col")
    x_hi = row // PLANES
    z = row % PLANES
    n_plane = (n_row // PLANES) * n_col
    place = x_hi * n_col + col

    def plane_device(slot):
        return ((slot // n_col) * PLANES + z, slot % n_col)

    def side_device(side):
        return ((row + side[0] + n_row) % n_row, (col + side[1] + n_col) % n_col)

    loads = []
    for n, (src, dst) in enumerate(((cen_h, cen_v), (rad_h, rad_v), (upp_h, upp_v), (obj_h, obj_v),
                                    (ker_h, ker_v), (low_h, low_v), (bia_h, bia_v))):
        copy = pltpu.make_async_copy(src, dst, load_sem.at[n])
        copy.start()
        loads.append(copy)

    barrier = pltpu.get_barrier_semaphore()
    greeted = 0
    for d in range(1, n_plane):
        pl.semaphore_signal(barrier, inc=1, device_id=plane_device((place + d) % n_plane), device_id_type=MESH)
        greeted += 1
    for d in range(1, PLANES):
        pl.semaphore_signal(barrier, inc=1, device_id=(x_hi * PLANES + (z + d) % PLANES, col), device_id_type=MESH)
        greeted += 1
    for side in SIDES:
        if side[0] != 0:
            pl.semaphore_signal(barrier, inc=1, device_id=side_device(side), device_id_type=MESH)
            greeted += 1

    zero_tile = jnp.zeros((8, 128), F32)

    def halo_start(n, src_ref, maps, deep, bufs):
        rows_src, cols_src, diag_src, rows_dst, cols_dst, diag_dst = bufs
        for m in range(maps):
            first = m * PAIRS * ROWS
            for r in range(deep):
                rows_src[UP, m, r] = src_ref[pl.ds(first + r, PAIRS, stride=ROWS), :]
                rows_src[DOWN, m, r] = src_ref[pl.ds(first + ROWS - deep + r, PAIRS, stride=ROWS), :]
            cols_src[0, m] = src_ref[first : first + ROWS, :]
            cols_src[1, m] = src_ref[first + (PAIRS - 1) * ROWS : first + PAIRS * ROWS, :]
            last = first + (PAIRS - 1) * ROWS
            diag_src[0, m] = src_ref[first : first + deep, :]
            diag_src[1, m] = src_ref[last : last + deep, :]
            diag_src[2, m] = src_ref[first + ROWS - deep : first + ROWS, :]
            diag_src[3, m] = src_ref[last + ROWS - deep : last + ROWS, :]
        copies = []
        for s in (4, 5, 6, 7, 0, 1, 2, 3):
            if s < 2:
                src, dst = rows_src.at[s], rows_dst.at[s]
            elif s < 4:
                src, dst = cols_src.at[s - 2], cols_dst.at[s - 2]
            else:
                src, dst = diag_src.at[s - 4], diag_dst.at[s - 4]
            copy = pltpu.make_async_remote_copy(
                src_ref=src, dst_ref=dst, send_sem=halo_send.at[n, s], recv_sem=halo_recv.at[n, s],
                device_id=side_device(SIDES[s]), device_id_type=MESH)
            copy.start()
            copies.append(copy)
        return copies

    no_above = row == 0
    no_below = row == n_row - 1
    no_left = col == 0
    no_right = col == n_col - 1

    def halo_place(dst_ref, maps, deep, tall, top, bufs):
        _, _, _, rows_dst, cols_dst, diag_dst = bufs

        def cut(gone, v):
            return jnp.where(gone, 0.0, v)

        for m in range(maps):
            first = m * EPAIRS * tall
            last = first + (EPAIRS - 1) * tall
            for r in range(deep):
                dst_ref[pl.ds(first + tall + top + ROWS + r, PAIRS, stride=tall), :] = cut(
                    no_below, rows_dst[0, m, r])
                dst_ref[pl.ds(first + tall + top - deep + r, PAIRS, stride=tall), :] = cut(
                    no_above, rows_dst[1, m, r])
            dst_ref[last + top : last + top + ROWS, :] = cut(no_right, cols_dst[0, m])
            dst_ref[first + top : first + top + ROWS, :] = cut(no_left, cols_dst[1, m])
            dst_ref[last + top + ROWS : last + top + ROWS + deep, :] = cut(
                jnp.logical_or(no_below, no_right), diag_dst[0, m])
            dst_ref[first + top + ROWS : first + top + ROWS + deep, :] = cut(
                jnp.logical_or(no_below, no_left), diag_dst[1, m])
            dst_ref[last + top - deep : last + top, :] = cut(
                jnp.logical_or(no_above, no_right), diag_dst[2, m])
            dst_ref[first + top - deep : first + top, :] = cut(
                jnp.logical_or(no_above, no_left), diag_dst[3, m])

    sends = []

    def sum_start(n, first_row, second_row):
        pay_a[n, 0:1] = first_row
        pay_a[n, 1:2] = second_row
        buf_a[n, place, 0:1] = first_row
        buf_a[n, place, 1:2] = second_row
        for d in range(1, n_plane):
            pltpu.make_async_remote_copy(
                src_ref=pay_a.at[n], dst_ref=buf_a.at[n, place], send_sem=a_send.at[n], recv_sem=a_recv.at[n],
                device_id=plane_device((place + d) % n_plane), device_id_type=MESH).start()

    def whole(buf, n, count, send, recv):
        part = buf.at[n, 0:count]
        return pltpu.make_async_remote_copy(
            src_ref=part, dst_ref=part, send_sem=send.at[n], recv_sem=recv.at[n],
            device_id=side_device((0, 1)), device_id_type=MESH)

    def sum_middle(n):
        whole(buf_a, n, n_plane - 1, a_send, a_recv).wait_recv()
        part = jnp.sum(buf_a[n], axis=0)
        pay_b[n] = part
        buf_b[n, z] = part
        for d in range(1, PLANES):
            pltpu.make_async_remote_copy(
                src_ref=pay_b.at[n], dst_ref=buf_b.at[n, z], send_sem=b_send.at[n], recv_sem=b_recv.at[n],
                device_id=(x_hi * PLANES + (z + d) % PLANES, col), device_id_type=MESH).start()

    def sum_end(n):
        whole(buf_b, n, PLANES - 1, b_send, b_recv).wait_recv()
        return jnp.sum(buf_b[n], axis=0)

    lane = lax.broadcasted_iota(jnp.int32, (EXT, 128), 1) < CH
    lane_w = lax.broadcasted_iota(jnp.int32, (WIDE, 128), 1) < CH

    def windows(src_ref, which, slot):
        def step(t, carry):
            a = pltpu.roll(src_ref[ext(which, t), :], CH, 1)
            b = pltpu.roll(src_ref[ext(which, t + 1), :], CH, 1)
            y_s[at((slot * EPAIRS + t) * EXT, EXT), :] = jnp.where(lane, a, b)
            for dh in range(3):
                hi, lo = split(y_s[pl.ds((slot * EPAIRS + t) * EXT + dh, ROWS), :])
                lhs_i[slot, 0, dh, pl.ds(pl.multiple_of(t * ROWS, ROWS), ROWS), :] = hi
                lhs_i[slot, 1, dh, pl.ds(pl.multiple_of(t * ROWS, ROWS), ROWS), :] = lo
            return carry
        lax.fori_loop(0, PAIRS + 1, step, 0)

    def conv(slot, weight):
        size = PAIRS * ROWS
        halves = []
        for part in range(2):
            tiles = []
            for dh in range(3):
                tiles.append(lhs_i[slot, part, dh, 0:size, :])
                tiles.append(lhs_i[slot, part, dh, ROWS : size + ROWS, :])
            halves.append(jnp.concatenate(tiles, axis=1))
        out = jnp.dot(jnp.concatenate(halves, axis=0), wts[weight], preferred_element_type=F32)
        total = (out[size:, 128:] + out[size:, :128]) + out[:size, 128:] + out[:size, :128]
        conv_out[at(slot * size, size), :] = total

    def windows_wide(m):
        first = m * EPAIRS * WIDE
        ybase = 0

        def form(t, left, right):
            y_s[at(ybase + t * WIDE, WIDE), :] = jnp.where(lane_w, left, right)

        def turned(p):
            return pltpu.roll(d_w[at(first + p * WIDE, WIDE), :], CH, 1)

        none = jnp.zeros((WIDE, 128), F32)
        form(0, none, turned(0))
        form(EPAIRS, turned(EPAIRS - 1), none)

        def step(t, carry):
            form(t, turned(t - 1), turned(t))
            return carry
        lax.fori_loop(1, EPAIRS, step, 0)

        def cast(t, carry):
            for dh in range(3):
                ys = [y_s[pl.ds(ybase + (2 * t + i) * WIDE + dh, EXT), :] for i in range(3)]
                for half in range(2):
                    hi, lo = split(jnp.concatenate([ys[half], ys[half + 1]], axis=0))
                    rows = pl.ds(pl.multiple_of(t * 2 * EXT, 16), 2 * EXT)
                    lhs_x[0, rows, (dh * 2 + half) * 128 : (dh * 2 + half + 1) * 128] = hi
                    lhs_x[1, rows, (dh * 2 + half) * 128 : (dh * 2 + half + 1) * 128] = lo
            return carry
        lax.fori_loop(0, EPAIRS // 2, cast, 0)

    def conv_wide(m):
        size = EPAIRS * EXT
        for part in range(2):
            out = jnp.dot(lhs_x[part], wts[3 + m], preferred_element_type=F32)
            total = out[:, 128:] + out[:, :128]
            if part == 0:
                upd[at(m * size, size), :] = total
            else:
                upd[at(m * size, size), :] += total

    for n in range(4):
        loads[n].wait()

    def fill(j, carry):
        lanes = pl.ds(pl.multiple_of(j * 128, 128), 128)
        c = cen_v[:, lanes].astype(F32)
        r = rad_v[:, lanes].astype(F32)
        lo, hi = c - r, c + r
        vals = {MID: 0.5 * (hi + lo), HALF: 0.5 * (hi - lo), OBJ: obj_v[:, lanes]}
        for m, name in enumerate((H1, H2, H3)):
            vals[name] = 0.5 * upp_v[m, :, lanes].astype(F32)
        for name, v in vals.items():
            base[inner(name, j), :] = v
            if name <= OBJ:
                wide_in[at((name * EPAIRS + j + 1) * EXT, 8), :] = zero_tile
                wide_in[at((name * EPAIRS + j + 1) * EXT + 16, 8), :] = zero_tile
                wide_in[ext_inner(name, j), :] = v
        return carry
    lax.fori_loop(0, PAIRS, fill, 0)
    for m in range(5):
        for e in (0, EPAIRS - 1):
            wide_in[ext(m, e), :] = jnp.zeros((EXT, 128), F32)

    pl.semaphore_wait(barrier, greeted)
    bufs0 = (rows_s0, cols_s0, diag_s0, rows_r0, cols_r0, diag_r0)
    first_copies = halo_start(0, base, 5, 1, bufs0)
    sends += first_copies

    for n in range(4, 7):
        loads[n].wait()

    def fill_low(j, carry):
        lanes = pl.ds(pl.multiple_of(j * 128, 128), 128)
        for m, name in enumerate((Q1, Q2, Q3)):
            base[inner(name, j), :] = 0.5 * low_v[m, :, lanes].astype(F32)
        return carry
    lax.fori_loop(0, PAIRS, fill_low, 0)

    bias = jnp.concatenate([bia_v[...], bia_v[...]], axis=1)
    none64 = jnp.zeros((CH, CH), F32)

    def put_weight(slot, dh, block):
        hi, lo = split(block)
        wts[slot, dh * 256 : (dh + 1) * 256, 0:128] = hi
        wts[slot, dh * 256 : (dh + 1) * 256, 128:256] = lo

    def build(k, carry):
        for dh in range(3):
            taps = [ker_v[k, 2 - dh, dw] for dw in range(3)]
            one = jnp.concatenate([jnp.concatenate([taps[2], taps[1]], axis=1),
                                   jnp.concatenate([none64, taps[2]], axis=1)], axis=0)
            two = jnp.concatenate([jnp.concatenate([taps[0], none64], axis=1),
                                   jnp.concatenate([taps[1], taps[0]], axis=1)], axis=0)
            put_weight(3 + k, dh, jnp.concatenate([one.T, two.T], axis=0))
        return carry
    lax.fori_loop(0, LAYERS, build, 0)

    def build_forward(k, carry):
        for dh in range(3):
            taps = [ker_v[k, dh, dw] for dw in range(3)]
            put_weight(k, dh, jnp.concatenate(
                [jnp.concatenate(taps + [none64], axis=0), jnp.concatenate([none64] + taps, axis=0)], axis=1))
        return carry
    lax.fori_loop(0, DEPTH, build_forward, 0)

    def clear(t, carry):
        d_w[at(t * WIDE, WIDE), :] = jnp.zeros((WIDE, 128), F32)
        return carry
    lax.fori_loop(0, DEPTH * EPAIRS, clear, 0)

    for copy in first_copies:
        copy.wait_recv()
    halo_place(wide_in, 5, 1, EXT, 1, bufs0)

    def value_terms(i, j):
        q = -0.5
        total = base[inner(OBJ, j), :] * bias[DEPTH : DEPTH + 1]
        mid, half = base[inner(MID, j), :], base[inner(HALF, j), :]
        hs = [base[inner(n, j), :] for n in (H1, H2, H3)]
        qs = [base[inner(n, j), :] for n in (Q1, Q2, Q3)]
        t3 = tb[inner(0, j), :]
        if i == 0:
            total += q * softplus(-4.0 * hs[2] * t3)
            return total
        g0 = g_x[ext_inner(0, j), :]
        total += g0 * (mid - half) + q * softplus(-4.0 * half * g0)
        lams = [lam_x[ext_inner(0, j), :], lam_x[ext_inner(1, j), :], lam[inner(0, j), :]]
        mus = [mu_x[ext_inner(0, j), :], mu_x[ext_inner(1, j), :], mu[inner(0, j), :]]
        for m in range(DEPTH):
            g = g_x[ext_inner(m + 1, j), :] if m < 2 else mus[2] + t3
            total += q * softplus(-4.0 * hs[m] * g)
            total += q * softplus(-4.0 * hs[m] * (lams[m] - mus[m]))
            total += q * softplus(4.0 * qs[m] * lams[m])
            total -= lams[m] * bias[m : m + 1]
        return total

    def value_row(i):
        def step(j, acc):
            return acc + value_terms(i, j)
        acc = lax.fori_loop(0, PAIRS, step, jnp.zeros((ROWS, 128), F32))
        out = jnp.sum(acc, axis=0, keepdims=True)
        if i == 0:
            out = out - (0.5 * 0.6931471805599453 * 9 * ROWS * PAIRS)
        return out

    scale = None
    value_prev = jnp.zeros((1, 128), F32)
    totals = []
    for i in range(ITERS):
        if i == 0:
            def start_x(e, carry):
                xs = [wide_in[ext(MID, e), :], wide_in[ext(H1, e), :], wide_in[ext(H2, e), :]]
                for k in range(DEPTH):
                    x_x[ext(k, e), :] = xs[k]
                for m in range(2):
                    p_x[ext(m, e), :] = xs[m + 1]
                    dmu_x[ext(m, e), :] = x_x[ext(m + 1, e), :] - p_x[ext(m, e), :]
                return carry
            lax.fori_loop(0, EPAIRS, start_x, 0)
            windows(wide_in, OBJ, 3)
            conv(3, 3 + DEPTH)

            def start_inner(j, carry):
                t3 = conv_out[inner(3, j), :]
                tb[inner(0, j), :] = t3
                hs = [base[inner(n, j), :] for n in (H1, H2, H3)]
                qs = [base[inner(n, j), :] for n in (Q1, Q2, Q3)]
                dmu[inner(0, j), :] = (hs[2] - hs[2] * jnp.tanh(2.0 * hs[2] * t3)) - hs[2]
                for m in range(DEPTH):
                    pn[inner(m, j), :] = hs[m] - qs[m] - bias[m : m + 1]
                return carry
            lax.fori_loop(0, PAIRS, start_inner, 0)
        else:
            first = i == 1

            def step_x(e, carry):
                halfs = [wide_in[ext(n, e), :] for n in (HALF, H1, H2)]
                mids = [wide_in[ext(MID, e), :], halfs[1], halfs[2]]
                xs = []
                mus = []
                for m in range(2):
                    new_mu = scale * dmu_x[ext(m, e), :]
                    new_lam = scale * d_w[pl.ds((m * EPAIRS + e) * WIDE + 1, EXT), :]
                    if not first:
                        new_mu = mu_x[ext(m, e), :] + new_mu
                        new_lam = lam_x[ext(m, e), :] + new_lam
                    mu_x[ext(m, e), :] = new_mu
                    lam_x[ext(m, e), :] = new_lam
                    mus.append((new_mu, new_lam))
                for k in range(DEPTH):
                    t = scale * upd[ext(k, e), :]
                    if not first:
                        t = trans[ext(k, e), :] + t
                    trans[ext(k, e), :] = t
                    g = -t if k == 0 else mus[k - 1][0] - t
                    g_x[ext(k, e), :] = g
                    x = mids[k] - halfs[k] * jnp.tanh(2.0 * halfs[k] * g)
                    x_x[ext(k, e), :] = x
                    xs.append(x)
                for m in range(2):
                    h = halfs[m + 1]
                    p = h - h * jnp.tanh(2.0 * h * (mus[m][1] - mus[m][0]))
                    p_x[ext(m, e), :] = p
                    dmu_x[ext(m, e), :] = xs[m + 1] - p
                return carry
            lax.fori_loop(0, EPAIRS, step_x, 0)

            def step_inner(j, carry):
                hs2 = base[inner(H3, j), :]
                qs = [base[inner(n, j), :] for n in (Q1, Q2, Q3)]
                new_mu = scale * dmu[inner(0, j), :]
                new_lam = scale * dl[inner(2, j), :]
                if not first:
                    new_mu = mu[inner(0, j), :] + new_mu
                    new_lam = lam[inner(0, j), :] + new_lam
                mu[inner(0, j), :] = new_mu
                lam[inner(0, j), :] = new_lam
                lams = [lam_x[ext_inner(0, j), :], lam_x[ext_inner(1, j), :], new_lam]
                p3 = hs2 - hs2 * jnp.tanh(2.0 * hs2 * (new_lam - new_mu))
                ps = [p_x[ext_inner(0, j), :], p_x[ext_inner(1, j), :], p3]
                g3 = new_mu + tb[inner(0, j), :]
                dmu[inner(0, j), :] = (hs2 - hs2 * jnp.tanh(2.0 * hs2 * g3)) - p3
                for m in range(DEPTH):
                    n = qs[m] + qs[m] * jnp.tanh(2.0 * qs[m] * lams[m])
                    pn[inner(m, j), :] = ps[m] - n - bias[m : m + 1]
                return carry
            lax.fori_loop(0, PAIRS, step_inner, 0)

        for k in range(DEPTH):
            windows(x_x, k, k)
            conv(k, k)

        def step_slope(j, acc):
            for m in range(DEPTH):
                v = pn[inner(m, j), :] - conv_out[inner(m, j), :]
                dl[inner(m, j), :] = v
                d_w[pl.ds((m * EPAIRS + j + 1) * WIDE + 2, ROWS), :] = v
                acc = acc + v * v
            for m in range(2):
                v = dmu_x[ext_inner(m, j), :]
                acc = acc + v * v
            v = dmu[inner(0, j), :]
            return acc + v * v
        acc = lax.fori_loop(0, PAIRS, step_slope, jnp.zeros((ROWS, 128), F32))
        sum_start(i, jnp.sum(acc, axis=0, keepdims=True), value_prev)

        copies = []
        if i < ITERS - 1:
            bufs = tuple(ref.at[i] for ref in (rows_s, cols_s, diag_s, rows_r, cols_r, diag_r))
            copies = halo_start(1 + i, dl, DEPTH, 2, bufs)
            sends += copies
        value_prev = value_row(i)
        sum_middle(i)
        if i < ITERS - 1:
            for copy in copies:
                copy.wait_recv()
            halo_place(d_w, DEPTH, 2, WIDE, 2, bufs)
            for m in range(DEPTH):
                windows_wide(m)
                conv_wide(m)
        else:
            sum_start(ITERS, jnp.zeros((1, 128), F32), value_prev)
        both = sum_end(i)
        squares = jnp.sum(both[0:1], axis=1, keepdims=True)
        scale = steps[i] / jnp.sqrt(squares / (2 * DEPTH * total_cells) + EPS)
        scale = jnp.broadcast_to(scale, (1, 128))
        totals.append(both)

    def finish(j, carry):
        lanes = pl.ds(pl.multiple_of(j * 128, 128), 128)
        for m in range(2):
            lam_out[m, :, lanes] = lam_x[ext_inner(m, j), :] + scale * dl[inner(m, j), :]
            mu_out[m, :, lanes] = mu_x[ext_inner(m, j), :] + scale * dmu_x[ext_inner(m, j), :]
        lam_out[2, :, lanes] = lam[inner(0, j), :] + scale * dl[inner(2, j), :]
        mu_out[2, :, lanes] = mu[inner(0, j), :] + scale * dmu[inner(0, j), :]
        return carry
    lax.fori_loop(0, PAIRS, finish, 0)
    sum_middle(ITERS)
    totals.append(sum_end(ITERS))
    for i in range(ITERS):
        bounds_ref[i] = jnp.sum(totals[i + 1][1:2]) / total_cells

    for copy in sends:
        copy.wait_send()
    for n in range(ITERS + 1):
        whole(buf_a, n, n_plane - 1, a_send, a_recv).wait_send()
        whole(buf_b, n, PLANES - 1, b_send, b_recv).wait_send()


def solution(mesh):
    n_row, n_col = mesh.shape["row"], mesh.shape["col"]
    n_plane = (n_row // PLANES) * n_col
    total_cells = n_row * n_col * ROWS * PAIRS * 128

    def vm(*shape, dtype=F32):
        return pltpu.VMEM(shape, dtype)

    inner_rows = PAIRS * ROWS
    ext_rows = EPAIRS * EXT
    lanes = PAIRS * 128
    any_spec = pl.BlockSpec(memory_space=pl.ANY)

    def kernel(*refs):
        body(float(total_cells), n_row, n_col, *refs)

    def shards(*args):
        call = pl.pallas_call(
            kernel,
            out_shape=(jax.ShapeDtypeStruct((ITERS,), F32),
                       jax.ShapeDtypeStruct((DEPTH, ROWS, lanes), F32),
                       jax.ShapeDtypeStruct((DEPTH, ROWS, lanes), F32)),
            in_specs=[any_spec] * 7 + [pl.BlockSpec(memory_space=pltpu.SMEM)],
            out_specs=(pl.BlockSpec(memory_space=pltpu.SMEM),
                       pl.BlockSpec(memory_space=pltpu.VMEM), pl.BlockSpec(memory_space=pltpu.VMEM)),
            scratch_shapes=[
                vm(ROWS, lanes), vm(ROWS, lanes, dtype=BF16), vm(ROWS, lanes, dtype=BF16),
                vm(DEPTH, ROWS, lanes, dtype=BF16), vm(DEPTH, ROWS, lanes, dtype=BF16),
                vm(LAYERS, 3, 3, CH, CH), vm(LAYERS, CH),
                vm(9 * inner_rows, 128), vm(5 * ext_rows, 128),
                vm(inner_rows, 128), vm(inner_rows, 128),
                vm(2 * ext_rows, 128), vm(2 * ext_rows, 128),
                vm(3 * inner_rows, 128), vm(inner_rows, 128), vm(2 * ext_rows, 128),
                vm(3 * ext_rows, 128), vm(3 * ext_rows, 128),
                vm(3 * ext_rows, 128), vm(3 * ext_rows, 128), vm(2 * ext_rows, 128),
                vm(3 * inner_rows, 128), vm(inner_rows, 128), vm(4 * inner_rows, 128),
                vm(3 * EPAIRS * WIDE, 128), vm(4 * ext_rows, 128),
                vm(4, 2, 3, inner_rows + ROWS, 128, dtype=BF16), vm(2, ext_rows, 768, dtype=BF16),
                vm(7, 768, 256, dtype=BF16),
                vm(2, 5, 1, PAIRS, 128), vm(2, 5, ROWS, 128), vm(4, 5, 1, 128),
                vm(2, 5, 1, PAIRS, 128), vm(2, 5, ROWS, 128), vm(4, 5, 1, 128),
                vm(2, 2, 3, 2, PAIRS, 128), vm(2, 2, 3, ROWS, 128), vm(2, 4, 3, 2, 128),
                vm(2, 2, 3, 2, PAIRS, 128), vm(2, 2, 3, ROWS, 128), vm(2, 4, 3, 2, 128),
                vm(ITERS + 1, 2, 128), vm(ITERS + 1, n_plane, 2, 128),
                vm(ITERS + 1, 2, 128), vm(ITERS + 1, PLANES, 2, 128),
                pltpu.SemaphoreType.DMA((7,)),
                pltpu.SemaphoreType.DMA((3, 8)), pltpu.SemaphoreType.DMA((3, 8)),
                pltpu.SemaphoreType.DMA((ITERS + 1,)), pltpu.SemaphoreType.DMA((ITERS + 1,)),
                pltpu.SemaphoreType.DMA((ITERS + 1,)), pltpu.SemaphoreType.DMA((ITERS + 1,)),
            ],
            compiler_params=pltpu.CompilerParams(
                collective_id=0, has_side_effects=True, vmem_limit_bytes=56 * 1024 * 1024),
            name="ascent",
        )
        return call(*args)

    placed = (P("row", "col"), P("row", "col"), P("row", "col"), P(None, "row", "col"), P(None, "row", "col"),
              P(), P(), P())
    return jax.shard_map(
        shards, mesh=mesh, in_specs=placed,
        out_specs=(P(), P(None, "row", "col"), P(None, "row", "col")), check_vma=False)
```

time: 675 us -> 82.2 us (0.12); the launches traced: 666 us -> 82 us
  blocking collectives: 254 us -> 0 us
  local copies, waits for them, and re-layouts: 125 us -> 4.62 us
  matrix products: 87.9 us -> 0 us
  Pallas kernels: 0 us -> 76.8 us
  starting transfers between devices: 71.9 us -> 0 us
  other arithmetic: 66.3 us -> 0 us
  between operations: 47.8 us -> 0.64 us
  waiting for transfers between devices: 13.5 us -> 0 us
    psum x3 -> x0, blocking collectives: 254 us -> none  [shards(): total_squares, total_value = lax.psum((squares, value), ('row', 'col'))]
    dot_general x171 -> x0, matrix products: 87.9 us -> none  [conv_valid(): jnp.dot(window, kernel[offset_row, offset_col], precision=lax.Precision.H...]
    pallas_call x0 -> x1, Pallas kernels: none -> 76.8 us  [shards(): return call(*args)]
    ppermute x28 -> x0, starting transfers between devices: 71.9 us -> none  [the longest x14 46.3 us: extended(): lax.ppermute(tail, axis, [(i, (i + 1) % count) for i in range(ends)])]
    squeeze x41 -> x0, local copies, waits for them, and re-layouts: 37.1 us -> none  [the longest x8 9.27 us: shards(): pos_coef = duals[j] - multipliers[j]]
    neg x19 -> x0, local copies, waits for them, and re-layouts: 25.3 us -> none  [the longest x15 21.6 us: shards(): coef = -conv_valid(dual_rim[layer], flipped(kernels[layer]))]
    reduce_sum x13 -> x0, other arithmetic: 23.2 us -> none  [the longest x3 6.8 us: shards(): jnp.sum(slope_mult * slope_mult)]
    sub x11 -> x0, other arithmetic: 18 us -> none  [the longest x7 13.1 us: shards(): slope_mult = points[j + 1] - positive]
  transfers between devices with their start and end apart: 28 -> 0, of which waited for: 7 -> 0; matrix products, arithmetic and copies ran while one was open for 15% -> 0% of each run, Pallas kernels for 0% -> 0%
where the time goes in v1:
time: 82.2 us; the launch traced here: 82 us
  Pallas kernels  76.8 us (93%)
  local copies, waits for them, and re-layouts  4.62 us (6%)
    pallas_call x1, Pallas kernels, shards(): return call(*args)  76.8 us
    unnamed x3, local copies, waits for them, and re-layouts  4.62 us

profile of v1, /device:TPU:1, one launch (start us, length us, event | category | flops | bytes accessed | tf_op | source)
XLA Modules:
  0.0 82.0 jit_solution(8699757109146239158)
XLA Ops:
  0.6 76.8 %ascent.1 = (f32[3]{0:T(128)}, f32[3,16,2048]{2,1,0:T(8,128)}, f32[3,16,2048]{2,1,0:T(8,128)}) custom-call(f32[16,2048]{1,0:T(8,128)} %refs_0_.1, bf16[16,2048]{1,0:T(8,128)(2,1)} %refs_1_.1, bf16[16,2048]{1,0:T(8,128)(2,1)} %refs_2_.1, bf16[3,16,2048]{2,1,0:T(8,128)(2,1)} %refs_3_.1, bf16[3,16,2048]{2,1,0:T(8,128)(2,1)} %refs_4_.1, ...), custom_call_target="tpu_custom_call" | custom-call | tf_op jit(solution)/shard_map/ascent/pallas_call | solution.py:559
  77.4 1.1 %copy.14 = f32[3]{0:T(128)} copy(f32[3]{0:T(128)} %get-tuple-element.6) | data formatting | bytes 24
  78.5 1.8 %copy.15 = f32[3,16,2048]{2,1,0:T(8,128)} copy(f32[3,16,2048]{2,1,0:T(8,128)} %get-tuple-element.7) | data formatting | bytes 786432
  80.3 1.8 %copy.16 = f32[3,16,2048]{2,1,0:T(8,128)} copy(f32[3,16,2048]{2,1,0:T(8,128)} %get-tuple-element.8) | data formatting | bytes 786432

commit v2 on v1

--- a/solution.py
+++ b/solution.py
@@ -53,8 +53,8 @@
 def body(total_cells, n_row, n_col, obj_h, cen_h, rad_h, low_h, upp_h, ker_h, bia_h, steps,
          bounds_ref, lam_out, mu_out,
          obj_v, cen_v, rad_v, low_v, upp_v, ker_v, bia_v,
-         base, wide_in, lam, mu, lam_x, mu_x, dl, dmu, dmu_x, trans, upd, g_x, x_x, p_x, pn, tb, conv_out,
-         d_w, y_s, lhs_i, lhs_x, wts,
+         base, wide_in, lam, mu, lam_x, mu_x, dl, dmu, dmu_x, trans, upd, g_x, p_x, pn, tb,
+         d_w, y_s, y_w, lhs_i, lhs_x, wts,
          rows_s0, cols_s0, diag_s0, rows_r0, cols_r0, diag_r0,
          rows_s, cols_s, diag_s, rows_r, cols_r, diag_r,
          pay_a, buf_a, pay_b, buf_b,
@@ -66,11 +66,17 @@
     n_plane = (n_row // PLANES) * n_col
     place = x_hi * n_col + col
 
-    def plane_device(slot):
-        return ((slot // n_col) * PLANES + z, slot % n_col)
+    def plane_device(d):
+        return (row ^ ((d // n_col) * PLANES), col ^ (d % n_col))
+
+    def line_device(d):
+        return (row ^ d, col)
+
+    ring = [[place_ for place_ in (at_, (at_ + 1) % size, (at_ + size - 1) % size)]
+            for at_, size in ((row, n_row), (col, n_col))]
 
     def side_device(side):
-        return ((row + side[0] + n_row) % n_row, (col + side[1] + n_col) % n_col)
+        return (ring[0][side[0]], ring[1][side[1]])
 
     loads = []
     for n, (src, dst) in enumerate(((cen_h, cen_v), (rad_h, rad_v), (upp_h, upp_v), (obj_h, obj_v),
@@ -82,10 +88,10 @@
     barrier = pltpu.get_barrier_semaphore()
     greeted = 0
     for d in range(1, n_plane):
-        pl.semaphore_signal(barrier, inc=1, device_id=plane_device((place + d) % n_plane), device_id_type=MESH)
+        pl.semaphore_signal(barrier, inc=1, device_id=plane_device(d), device_id_type=MESH)
         greeted += 1
     for d in range(1, PLANES):
-        pl.semaphore_signal(barrier, inc=1, device_id=(x_hi * PLANES + (z + d) % PLANES, col), device_id_type=MESH)
+        pl.semaphore_signal(barrier, inc=1, device_id=line_device(d), device_id_type=MESH)
         greeted += 1
     for side in SIDES:
         if side[0] != 0:
@@ -128,14 +134,14 @@
     no_left = col == 0
     no_right = col == n_col - 1
 
-    def halo_place(dst_ref, maps, deep, tall, top, bufs):
+    def halo_place(dst_ref, maps, deep, tall, top, pairs, bufs):
         _, _, _, rows_dst, cols_dst, diag_dst = bufs
 
         def cut(gone, v):
             return jnp.where(gone, 0.0, v)
 
         for m in range(maps):
-            first = m * EPAIRS * tall
+            first = m * pairs * tall
             last = first + (EPAIRS - 1) * tall
             for r in range(deep):
                 dst_ref[pl.ds(first + tall + top + ROWS + r, PAIRS, stride=tall), :] = cut(
@@ -163,7 +169,7 @@
         for d in range(1, n_plane):
             pltpu.make_async_remote_copy(
                 src_ref=pay_a.at[n], dst_ref=buf_a.at[n, place], send_sem=a_send.at[n], recv_sem=a_recv.at[n],
-                device_id=plane_device((place + d) % n_plane), device_id_type=MESH).start()
+                device_id=plane_device(d), device_id_type=MESH).start()
 
     def whole(buf, n, count, send, recv):
         part = buf.at[n, 0:count]
@@ -179,7 +185,7 @@
         for d in range(1, PLANES):
             pltpu.make_async_remote_copy(
                 src_ref=pay_b.at[n], dst_ref=buf_b.at[n, z], send_sem=b_send.at[n], recv_sem=b_recv.at[n],
-                device_id=(x_hi * PLANES + (z + d) % PLANES, col), device_id_type=MESH).start()
+                device_id=line_device(d), device_id_type=MESH).start()
 
     def sum_end(n):
         whole(buf_b, n, PLANES - 1, b_send, b_recv).wait_recv()
@@ -188,17 +194,17 @@
     lane = lax.broadcasted_iota(jnp.int32, (EXT, 128), 1) < CH
     lane_w = lax.broadcasted_iota(jnp.int32, (WIDE, 128), 1) < CH
 
-    def windows(src_ref, which, slot):
-        def step(t, carry):
-            a = pltpu.roll(src_ref[ext(which, t), :], CH, 1)
-            b = pltpu.roll(src_ref[ext(which, t + 1), :], CH, 1)
-            y_s[at((slot * EPAIRS + t) * EXT, EXT), :] = jnp.where(lane, a, b)
-            for dh in range(3):
-                hi, lo = split(y_s[pl.ds((slot * EPAIRS + t) * EXT + dh, ROWS), :])
-                lhs_i[slot, 0, dh, pl.ds(pl.multiple_of(t * ROWS, ROWS), ROWS), :] = hi
-                lhs_i[slot, 1, dh, pl.ds(pl.multiple_of(t * ROWS, ROWS), ROWS), :] = lo
-            return carry
-        lax.fori_loop(0, PAIRS + 1, step, 0)
+    def turn(x):
+        return pltpu.roll(x, CH, 1)
+
+    def window(k, u, e, before, now):
+        y = y_s[u * LAYERS + k]
+        y[...] = jnp.where(lane, before, now)
+        for dh in range(3):
+            hi, lo = split(y[dh : dh + ROWS, :])
+            rows = pl.ds(pl.multiple_of(e * ROWS, ROWS), ROWS)
+            lhs_i[k, 0, dh, rows, :] = hi
+            lhs_i[k, 1, dh, rows, :] = lo
 
     def conv(slot, weight):
         size = PAIRS * ROWS
@@ -206,52 +212,48 @@
         for part in range(2):
             tiles = []
             for dh in range(3):
-                tiles.append(lhs_i[slot, part, dh, 0:size, :])
                 tiles.append(lhs_i[slot, part, dh, ROWS : size + ROWS, :])
+                tiles.append(lhs_i[slot, part, dh, 2 * ROWS : size + 2 * ROWS, :])
             halves.append(jnp.concatenate(tiles, axis=1))
-        out = jnp.dot(jnp.concatenate(halves, axis=0), wts[weight], preferred_element_type=F32)
-        total = (out[size:, 128:] + out[size:, :128]) + out[:size, 128:] + out[:size, :128]
-        conv_out[at(slot * size, size), :] = total
-
-    def windows_wide(m):
-        first = m * EPAIRS * WIDE
-        ybase = 0
-
-        def form(t, left, right):
-            y_s[at(ybase + t * WIDE, WIDE), :] = jnp.where(lane_w, left, right)
-
-        def turned(p):
-            return pltpu.roll(d_w[at(first + p * WIDE, WIDE), :], CH, 1)
+        high = jnp.dot(halves[0], wts[weight], preferred_element_type=F32)
+        low = jnp.dot(halves[1], wts[weight, :, 0:128], preferred_element_type=F32)
+        return (low + high[:, 128:]) + high[:, :128]
+
+    def windows_wide():
+        def wide(m, p):
+            return turn(d_w[at((m * (EPAIRS + 1) + p) * WIDE, WIDE), :])
 
         none = jnp.zeros((WIDE, 128), F32)
-        form(0, none, turned(0))
-        form(EPAIRS, turned(EPAIRS - 1), none)
+        start = []
+        for m in range(DEPTH):
+            r = wide(m, 0)
+            start += [r, jnp.where(lane_w, none, r)]
 
         def step(t, carry):
-            form(t, turned(t - 1), turned(t))
-            return carry
-        lax.fori_loop(1, EPAIRS, step, 0)
-
-        def cast(t, carry):
-            for dh in range(3):
-                ys = [y_s[pl.ds(ybase + (2 * t + i) * WIDE + dh, EXT), :] for i in range(3)]
-                for half in range(2):
-                    hi, lo = split(jnp.concatenate([ys[half], ys[half + 1]], axis=0))
-                    rows = pl.ds(pl.multiple_of(t * 2 * EXT, 16), 2 * EXT)
-                    lhs_x[0, rows, (dh * 2 + half) * 128 : (dh * 2 + half + 1) * 128] = hi
-                    lhs_x[1, rows, (dh * 2 + half) * 128 : (dh * 2 + half + 1) * 128] = lo
-            return carry
-        lax.fori_loop(0, EPAIRS // 2, cast, 0)
+            out = []
+            for m in range(DEPTH):
+                r0, ya = carry[2 * m], carry[2 * m + 1]
+                r1, r2 = wide(m, 2 * t + 1), wide(m, 2 * t + 2)
+                yb = jnp.where(lane_w, r0, r1)
+                yc = jnp.where(lane_w, r1, r2)
+                for i, y in enumerate((ya, yb, yc)):
+                    y_w[m * 3 + i][...] = y
+                for dh in range(3):
+                    ys = [y_w[m * 3 + i][dh : dh + EXT, :] for i in range(3)]
+                    for half in range(2):
+                        hi, lo = split(jnp.concatenate([ys[half], ys[half + 1]], axis=0))
+                        rows = pl.ds(pl.multiple_of(t * 2 * EXT, 16), 2 * EXT)
+                        lhs_x[m, 0, rows, (dh * 2 + half) * 128 : (dh * 2 + half + 1) * 128] = hi
+                        lhs_x[m, 1, rows, (dh * 2 + half) * 128 : (dh * 2 + half + 1) * 128] = lo
+                out += [r2, yc]
+            return tuple(out)
+        lax.fori_loop(0, EPAIRS // 2, step, tuple(start))
 
     def conv_wide(m):
         size = EPAIRS * EXT
-        for part in range(2):
-            out = jnp.dot(lhs_x[part], wts[3 + m], preferred_element_type=F32)
-            total = out[:, 128:] + out[:, :128]
-            if part == 0:
-                upd[at(m * size, size), :] = total
-            else:
-                upd[at(m * size, size), :] += total
+        high = jnp.dot(lhs_x[m, 0], wts[3 + m], preferred_element_type=F32)
+        low = jnp.dot(lhs_x[m, 1], wts[3 + m, :, 0:128], preferred_element_type=F32)
+        upd[at(m * size, size), :] = (low + high[:, 128:]) + high[:, :128]
 
     for n in range(4):
         loads[n].wait()
@@ -321,11 +323,11 @@
     def clear(t, carry):
         d_w[at(t * WIDE, WIDE), :] = jnp.zeros((WIDE, 128), F32)
         return carry
-    lax.fori_loop(0, DEPTH * EPAIRS, clear, 0)
+    lax.fori_loop(0, DEPTH * (EPAIRS + 1), clear, 0)
 
     for copy in first_copies:
         copy.wait_recv()
-    halo_place(wide_in, 5, 1, EXT, 1, bufs0)
+    halo_place(wide_in, 5, 1, EXT, 1, EPAIRS, bufs0)
 
     def value_terms(i, j):
         q = -0.5
@@ -362,101 +364,92 @@
     value_prev = jnp.zeros((1, 128), F32)
     totals = []
     for i in range(ITERS):
+        first = i == 1
+
+        def step_x(g, carry):
+            before = list(carry)
+            for u in range(3):
+                e = 3 * g + u
+                if i == 0:
+                    xs = [wide_in[ext(n, e), :] for n in (MID, H1, H2)]
+                    for m in range(2):
+                        p_x[ext(m, e), :] = xs[m + 1]
+                        dmu_x[ext(m, e), :] = xs[m + 1] - p_x[ext(m, e), :]
+                    xs.append(wide_in[ext(OBJ, e), :])
+                else:
+                    halfs = [wide_in[ext(n, e), :] for n in (HALF, H1, H2)]
+                    mids = [wide_in[ext(MID, e), :], halfs[1], halfs[2]]
+                    xs = []
+                    mus = []
+                    for m in range(2):
+                        new_mu = scale * dmu_x[ext(m, e), :]
+                        new_lam = scale * d_w[pl.ds((m * (EPAIRS + 1) + e) * WIDE + 1, EXT), :]
+                        if not first:
+                            new_mu = mu_x[ext(m, e), :] + new_mu
+                            new_lam = lam_x[ext(m, e), :] + new_lam
+                        mu_x[ext(m, e), :] = new_mu
+                        lam_x[ext(m, e), :] = new_lam
+                        mus.append((new_mu, new_lam))
+                    for k in range(DEPTH):
+                        t = scale * upd[ext(k, e), :]
+                        if not first:
+                            t = trans[ext(k, e), :] + t
+                        trans[ext(k, e), :] = t
+                        coef = -t if k == 0 else mus[k - 1][0] - t
+                        g_x[ext(k, e), :] = coef
+                        xs.append(mids[k] - halfs[k] * jnp.tanh(2.0 * halfs[k] * coef))
+                    for m in range(2):
+                        h = halfs[m + 1]
+                        p = h - h * jnp.tanh(2.0 * h * (mus[m][1] - mus[m][0]))
+                        p_x[ext(m, e), :] = p
+                        dmu_x[ext(m, e), :] = xs[m + 1] - p
+                for k, x in enumerate(xs):
+                    now = turn(x)
+                    window(k, u, e, before[k], now)
+                    before[k] = now
+            return tuple(before)
+        maps = LAYERS if i == 0 else DEPTH
+        lax.fori_loop(0, EPAIRS // 3, step_x, tuple(jnp.zeros((EXT, 128), F32) for _ in range(maps)))
+
+        acc = jnp.zeros((ROWS, 128), F32)
         if i == 0:
-            def start_x(e, carry):
-                xs = [wide_in[ext(MID, e), :], wide_in[ext(H1, e), :], wide_in[ext(H2, e), :]]
-                for k in range(DEPTH):
-                    x_x[ext(k, e), :] = xs[k]
-                for m in range(2):
-                    p_x[ext(m, e), :] = xs[m + 1]
-                    dmu_x[ext(m, e), :] = x_x[ext(m + 1, e), :] - p_x[ext(m, e), :]
-                return carry
-            lax.fori_loop(0, EPAIRS, start_x, 0)
-            windows(wide_in, OBJ, 3)
-            conv(3, 3 + DEPTH)
-
-            def start_inner(j, carry):
-                t3 = conv_out[inner(3, j), :]
-                tb[inner(0, j), :] = t3
-                hs = [base[inner(n, j), :] for n in (H1, H2, H3)]
-                qs = [base[inner(n, j), :] for n in (Q1, Q2, Q3)]
-                dmu[inner(0, j), :] = (hs[2] - hs[2] * jnp.tanh(2.0 * hs[2] * t3)) - hs[2]
-                for m in range(DEPTH):
-                    pn[inner(m, j), :] = hs[m] - qs[m] - bias[m : m + 1]
-                return carry
-            lax.fori_loop(0, PAIRS, start_inner, 0)
-        else:
-            first = i == 1
-
-            def step_x(e, carry):
-                halfs = [wide_in[ext(n, e), :] for n in (HALF, H1, H2)]
-                mids = [wide_in[ext(MID, e), :], halfs[1], halfs[2]]
-                xs = []
-                mus = []
-                for m in range(2):
-                    new_mu = scale * dmu_x[ext(m, e), :]
-                    new_lam = scale * d_w[pl.ds((m * EPAIRS + e) * WIDE + 1, EXT), :]
-                    if not first:
-                        new_mu = mu_x[ext(m, e), :] + new_mu
-                        new_lam = lam_x[ext(m, e), :] + new_lam
-                    mu_x[ext(m, e), :] = new_mu
-                    lam_x[ext(m, e), :] = new_lam
-                    mus.append((new_mu, new_lam))
-                for k in range(DEPTH):
-                    t = scale * upd[ext(k, e), :]
-                    if not first:
-                        t = trans[ext(k, e), :] + t
-                    trans[ext(k, e), :] = t
-                    g = -t if k == 0 else mus[k - 1][0] - t
-                    g_x[ext(k, e), :] = g
-                    x = mids[k] - halfs[k] * jnp.tanh(2.0 * halfs[k] * g)
-                    x_x[ext(k, e), :] = x
-                    xs.append(x)
-                for m in range(2):
-                    h = halfs[m + 1]
-                    p = h - h * jnp.tanh(2.0 * h * (mus[m][1] - mus[m][0]))
-                    p_x[ext(m, e), :] = p
-                    dmu_x[ext(m, e), :] = xs[m + 1] - p
-                return carry
-            lax.fori_loop(0, EPAIRS, step_x, 0)
-
-            def step_inner(j, carry):
-                hs2 = base[inner(H3, j), :]
-                qs = [base[inner(n, j), :] for n in (Q1, Q2, Q3)]
-                new_mu = scale * dmu[inner(0, j), :]
-                new_lam = scale * dl[inner(2, j), :]
-                if not first:
-                    new_mu = mu[inner(0, j), :] + new_mu
-                    new_lam = lam[inner(0, j), :] + new_lam
-                mu[inner(0, j), :] = new_mu
-                lam[inner(0, j), :] = new_lam
-                lams = [lam_x[ext_inner(0, j), :], lam_x[ext_inner(1, j), :], new_lam]
-                p3 = hs2 - hs2 * jnp.tanh(2.0 * hs2 * (new_lam - new_mu))
-                ps = [p_x[ext_inner(0, j), :], p_x[ext_inner(1, j), :], p3]
-                g3 = new_mu + tb[inner(0, j), :]
-                dmu[inner(0, j), :] = (hs2 - hs2 * jnp.tanh(2.0 * hs2 * g3)) - p3
-                for m in range(DEPTH):
-                    n = qs[m] + qs[m] * jnp.tanh(2.0 * qs[m] * lams[m])
-                    pn[inner(m, j), :] = ps[m] - n - bias[m : m + 1]
-                return carry
-            lax.fori_loop(0, PAIRS, step_inner, 0)
-
-        for k in range(DEPTH):
-            windows(x_x, k, k)
-            conv(k, k)
-
-        def step_slope(j, acc):
-            for m in range(DEPTH):
-                v = pn[inner(m, j), :] - conv_out[inner(m, j), :]
+            back = conv(DEPTH, 3 + DEPTH)
+            for j in range(PAIRS):
+                tb[inner(0, j), :] = back[j * ROWS : (j + 1) * ROWS]
+        for m in (2, 0, 1):
+            rest = []
+            for j in range(PAIRS):
+                h = base[inner(H1 + m if m < 2 else H3, j), :]
+                q = base[inner(Q1 + m, j), :]
+                if m == 2:
+                    t3 = tb[inner(0, j), :]
+                    if i == 0:
+                        p, v_lam = h, None
+                    else:
+                        new_mu = scale * dmu[inner(0, j), :]
+                        v_lam = scale * dl[inner(2, j), :]
+                        if not first:
+                            new_mu = mu[inner(0, j), :] + new_mu
+                            v_lam = lam[inner(0, j), :] + v_lam
+                        mu[inner(0, j), :] = new_mu
+                        lam[inner(0, j), :] = v_lam
+                        p = h - h * jnp.tanh(2.0 * h * (v_lam - new_mu))
+                        t3 = new_mu + t3
+                    v = (h - h * jnp.tanh(2.0 * h * t3)) - p
+                    dmu[inner(0, j), :] = v
+                else:
+                    p = p_x[ext_inner(m, j), :]
+                    v_lam = None if i == 0 else lam_x[ext_inner(m, j), :]
+                    v = dmu_x[ext_inner(m, j), :]
+                acc = acc + v * v
+                n = q if i == 0 else q + q * jnp.tanh(2.0 * q * v_lam)
+                pn[inner(m, j), :] = p - n - bias[m : m + 1]
+            image = conv(m, m)
+            for j in range(PAIRS):
+                v = pn[inner(m, j), :] - image[j * ROWS : (j + 1) * ROWS]
                 dl[inner(m, j), :] = v
-                d_w[pl.ds((m * EPAIRS + j + 1) * WIDE + 2, ROWS), :] = v
+                d_w[pl.ds((m * (EPAIRS + 1) + j + 1) * WIDE + 2, ROWS), :] = v
                 acc = acc + v * v
-            for m in range(2):
-                v = dmu_x[ext_inner(m, j), :]
-                acc = acc + v * v
-            v = dmu[inner(0, j), :]
-            return acc + v * v
-        acc = lax.fori_loop(0, PAIRS, step_slope, jnp.zeros((ROWS, 128), F32))
         sum_start(i, jnp.sum(acc, axis=0, keepdims=True), value_prev)
 
         copies = []
@@ -469,9 +462,9 @@
         if i < ITERS - 1:
             for copy in copies:
                 copy.wait_recv()
-            halo_place(d_w, DEPTH, 2, WIDE, 2, bufs)
+            halo_place(d_w, DEPTH, 2, WIDE, 2, EPAIRS + 1, bufs)
+            windows_wide()
             for m in range(DEPTH):
-                windows_wide(m)
                 conv_wide(m)
         else:
             sum_start(ITERS, jnp.zeros((1, 128), F32), value_prev)
@@ -536,10 +529,11 @@
                 vm(2 * ext_rows, 128), vm(2 * ext_rows, 128),
                 vm(3 * inner_rows, 128), vm(inner_rows, 128), vm(2 * ext_rows, 128),
                 vm(3 * ext_rows, 128), vm(3 * ext_rows, 128),
-                vm(3 * ext_rows, 128), vm(3 * ext_rows, 128), vm(2 * ext_rows, 128),
-                vm(3 * inner_rows, 128), vm(inner_rows, 128), vm(4 * inner_rows, 128),
-                vm(3 * EPAIRS * WIDE, 128), vm(4 * ext_rows, 128),
-                vm(4, 2, 3, inner_rows + ROWS, 128, dtype=BF16), vm(2, ext_rows, 768, dtype=BF16),
+                vm(3 * ext_rows, 128), vm(2 * ext_rows, 128),
+                vm(3 * inner_rows, 128), vm(inner_rows, 128),
+                vm(3 * (EPAIRS + 1) * WIDE, 128),
+                [vm(EXT, 128)] * 12, [vm(WIDE, 128)] * 9,
+                vm(4, 2, 3, inner_rows + 2 * ROWS, 128, dtype=BF16), vm(3, 2, ext_rows, 768, dtype=BF16),
                 vm(7, 768, 256, dtype=BF16),
                 vm(2, 5, 1, PAIRS, 128), vm(2, 5, ROWS, 128), vm(4, 5, 1, 128),
                 vm(2, 5, 1, PAIRS, 128), vm(2, 5, ROWS, 128), vm(4, 5, 1, 128),

time: 82.2 us -> 60.5 us (0.74)
  Pallas kernels: 76.8 us -> 55.1 us
    pallas_call x1, Pallas kernels: 76.8 us -> 55.1 us  [shards(): return call(*args)]
where the time goes in v2:
time: 60.5 us; the launch traced here: 60.3 us
  Pallas kernels  55.1 us (91%)
  local copies, waits for them, and re-layouts  4.62 us (8%)
  between operations  0.64 us (1%)
    pallas_call x1, Pallas kernels, shards(): return call(*args)  55.1 us
    unnamed x3, local copies, waits for them, and re-layouts  4.62 us

profile of v2, /device:TPU:1, one launch (start us, length us, event | category | flops | bytes accessed | tf_op | source)
XLA Modules:
  0.0 60.3 jit_solution(11157235251940181703)
XLA Ops:
  0.6 55.1 %ascent.1 = (f32[3]{0:T(128)}, f32[3,16,2048]{2,1,0:T(8,128)}, f32[3,16,2048]{2,1,0:T(8,128)}) custom-call(f32[16,2048]{1,0:T(8,128)} %refs_0_.1, bf16[16,2048]{1,0:T(8,128)(2,1)} %refs_1_.1, bf16[16,2048]{1,0:T(8,128)(2,1)} %refs_2_.1, bf16[3,16,2048]{2,1,0:T(8,128)(2,1)} %refs_3_.1, bf16[3,16,2048]{2,1,0:T(8,128)(2,1)} %refs_4_.1, ...), custom_call_target="tpu_custom_call" | custom-call | tf_op jit(solution)/shard_map/ascent/pallas_call | solution.py:553
  55.7 1.1 %copy.14 = f32[3]{0:T(128)} copy(f32[3]{0:T(128)} %get-tuple-element.6) | data formatting | bytes 24
  56.8 1.8 %copy.15 = f32[3,16,2048]{2,1,0:T(8,128)} copy(f32[3,16,2048]{2,1,0:T(8,128)} %get-tuple-element.7) | data formatting | bytes 786432
  58.6 1.8 %copy.16 = f32[3,16,2048]{2,1,0:T(8,128)} copy(f32[3,16,2048]{2,1,0:T(8,128)} %get-tuple-element.8) | data formatting | bytes 786432

commit v3 on v2

--- a/solution.py
+++ b/solution.py
@@ -458,6 +458,8 @@
             copies = halo_start(1 + i, dl, DEPTH, 2, bufs)
             sends += copies
         value_prev = value_row(i)
+        if i == ITERS - 1:
+            sum_start(ITERS, jnp.zeros((1, 128), F32), value_prev)
         sum_middle(i)
         if i < ITERS - 1:
             for copy in copies:
@@ -467,7 +469,7 @@
             for m in range(DEPTH):
                 conv_wide(m)
         else:
-            sum_start(ITERS, jnp.zeros((1, 128), F32), value_prev)
+            sum_middle(ITERS)
         both = sum_end(i)
         squares = jnp.sum(both[0:1], axis=1, keepdims=True)
         scale = steps[i] / jnp.sqrt(squares / (2 * DEPTH * total_cells) + EPS)
@@ -483,10 +485,10 @@
         mu_out[2, :, lanes] = mu[inner(0, j), :] + scale * dmu[inner(0, j), :]
         return carry
     lax.fori_loop(0, PAIRS, finish, 0)
-    sum_middle(ITERS)
     totals.append(sum_end(ITERS))
     for i in range(ITERS):
-        bounds_ref[i] = jnp.sum(totals[i + 1][1:2]) / total_cells
+        mean = jnp.sum(totals[i + 1][1:2], axis=1, keepdims=True) / total_cells
+        bounds_ref[i : i + 1, :] = jnp.broadcast_to(mean, (1, 128))
 
     for copy in sends:
         copy.wait_send()
@@ -495,6 +497,16 @@
         whole(buf_b, n, PLANES - 1, b_send, b_recv).wait_send()
 
 
+def store(bounds_v, lam_v, mu_v, bounds_out, lam_out, mu_out, sem):
+    copies = [pltpu.make_async_copy(lam_v, lam_out, sem.at[0]), pltpu.make_async_copy(mu_v, mu_out, sem.at[1])]
+    for copy in copies:
+        copy.start()
+    for i in range(ITERS):
+        bounds_out[i] = bounds_v[i, 0]
+    for copy in copies:
+        copy.wait()
+
+
 def solution(mesh):
     n_row, n_col = mesh.shape["row"], mesh.shape["col"]
     n_plane = (n_row // PLANES) * n_col
@@ -506,7 +518,8 @@
     inner_rows = PAIRS * ROWS
     ext_rows = EPAIRS * EXT
     lanes = PAIRS * 128
-    any_spec = pl.BlockSpec(memory_space=pl.ANY)
+    hbm_spec = pl.BlockSpec(memory_space=pltpu.HBM)
+    vmem_spec = pl.BlockSpec(memory_space=pltpu.VMEM)
 
     def kernel(*refs):
         body(float(total_cells), n_row, n_col, *refs)
@@ -514,11 +527,11 @@
     def shards(*args):
         call = pl.pallas_call(
             kernel,
-            out_shape=(jax.ShapeDtypeStruct((ITERS,), F32),
-                       jax.ShapeDtypeStruct((DEPTH, ROWS, lanes), F32),
-                       jax.ShapeDtypeStruct((DEPTH, ROWS, lanes), F32)),
-            in_specs=[any_spec] * 7 + [pl.BlockSpec(memory_space=pltpu.SMEM)],
-            out_specs=(pl.BlockSpec(memory_space=pltpu.SMEM),
+            out_shape=(pltpu.VMEM((8, 128), F32),
+                       pltpu.VMEM((DEPTH, ROWS, lanes), F32),
+                       pltpu.VMEM((DEPTH, ROWS, lanes), F32)),
+            in_specs=[hbm_spec] * 7 + [pl.BlockSpec(memory_space=pltpu.SMEM)],
+            out_specs=(pl.BlockSpec(memory_space=pltpu.VMEM),
                        pl.BlockSpec(memory_space=pltpu.VMEM), pl.BlockSpec(memory_space=pltpu.VMEM)),
             scratch_shapes=[
                 vm(ROWS, lanes), vm(ROWS, lanes, dtype=BF16), vm(ROWS, lanes, dtype=BF16),
@@ -550,7 +563,18 @@
                 collective_id=0, has_side_effects=True, vmem_limit_bytes=56 * 1024 * 1024),
             name="ascent",
         )
-        return call(*args)
+        results = call(*args)
+        return pl.pallas_call(
+            store,
+            out_shape=(jax.ShapeDtypeStruct((ITERS,), F32),
+                       jax.ShapeDtypeStruct((DEPTH, ROWS, lanes), F32),
+                       jax.ShapeDtypeStruct((DEPTH, ROWS, lanes), F32)),
+            in_specs=[vmem_spec] * 3,
+            out_specs=(pl.BlockSpec(memory_space=pltpu.SMEM), hbm_spec, hbm_spec),
+            scratch_shapes=[pltpu.SemaphoreType.DMA((2,))],
+            compiler_params=pltpu.CompilerParams(vmem_limit_bytes=1024 * 1024),
+            name="store",
+        )(*results)
 
     placed = (P("row", "col"), P("row", "col"), P("row", "col"), P(None, "row", "col"), P(None, "row", "col"),
               P(), P(), P())

time: 60.5 us -> 52.6 us (0.87)
  local copies, waits for them, and re-layouts: 4.62 us -> 0 us
  Pallas kernels: 55.1 us -> 51.8 us
    unnamed x3 -> x0, local copies, waits for them, and re-layouts: 4.62 us -> none
    pallas_call x1 -> x2, Pallas kernels: 55.1 us -> 51.8 us  [the longest x1 50.4 us: shards(): results = call(*args)]
where the time goes in v3:
time: 52.6 us; the launch traced here: 52.5 us
  Pallas kernels  51.8 us (98%)
  between operations  0.64 us (1%)
    pallas_call x1, Pallas kernels, shards(): results = call(*args)  50.4 us
    pallas_call x1, Pallas kernels, shards(): pl.pallas_call(store, out_shape=(jax.ShapeDtypeStruct((ITERS,), F32), jax...  1.41 us

profile of v3, /device:TPU:1, one launch (start us, length us, event | category | flops | bytes accessed | tf_op | source)
XLA Modules:
  0.0 52.5 jit_solution(13397735942273106457)
XLA Ops:
  0.6 50.4 %ascent.1 = (f32[8,128]{1,0:T(8,128)S(1)}, f32[3,16,2048]{2,1,0:T(8,128)S(1)}, f32[3,16,2048]{2,1,0:T(8,128)S(1)}) custom-call(f32[16,2048]{1,0:T(8,128)} %refs_0_.1, bf16[16,2048]{1,0:T(8,128)(2,1)} %refs_1_.1, bf16[16,2048]{1,0:T(8,128)(2,1)} %refs_2_.1, bf16[3,16,2048]{2,1,0:T(8,128)(2,1)} %refs_3_.1, bf16[3,16,2048]{2,1,0:T(8,128)(2,1)} %refs_4_.1, ...), custom_call_target="tpu_custom_call" | custom-call | tf_op jit(solution)/shard_map/ascent/pallas_call | solution.py:566
  51.1 1.4 %store.1 = (f32[3]{0:T(128)}, f32[3,16,2048]{2,1,0:T(8,128)}, f32[3,16,2048]{2,1,0:T(8,128)}) custom-call(f32[8,128]{1,0:T(8,128)S(1)} %get-tuple-element.6.bounds_v, f32[3,16,2048]{2,1,0:T(8,128)S(1)} %get-tuple-element.7.lam_v, f32[3,16,2048]{2,1,0:T(8,128)S(1)} %get-tuple-element.8.mu_v), custom_call_target="tpu_custom_call" | custom-call | tf_op jit(solution)/shard_map/store/pallas_call | solution.py:567

commit v4 on v3

--- a/solution.py
+++ b/solution.py
@@ -41,10 +41,6 @@
     return pl.ds((which * EPAIRS + pair + 1) * EXT + 1, ROWS)
 
 
-def softplus(z):
-    return jnp.maximum(z, 0.0) + jnp.log1p(jnp.exp(-jnp.abs(z)))
-
-
 def split(v):
     hi = v.astype(BF16)
     return hi, (v - hi.astype(F32)).astype(BF16)
@@ -53,24 +49,17 @@
 def body(total_cells, n_row, n_col, obj_h, cen_h, rad_h, low_h, upp_h, ker_h, bia_h, steps,
          bounds_ref, lam_out, mu_out,
          obj_v, cen_v, rad_v, low_v, upp_v, ker_v, bia_v,
-         base, wide_in, lam, mu, lam_x, mu_x, dl, dmu, dmu_x, trans, upd, g_x, p_x, pn, tb,
+         base, wide_in, lam, mu, lam_x, mu_x, dl, dmu, dmu_x, trans, upd, p_x, pn, tb,
          d_w, y_s, y_w, lhs_i, lhs_x, wts,
          rows_s0, cols_s0, diag_s0, rows_r0, cols_r0, diag_r0,
          rows_s, cols_s, diag_s, rows_r, cols_r, diag_r,
-         pay_a, buf_a, pay_b, buf_b,
-         load_sem, halo_send, halo_recv, a_send, a_recv, b_send, b_recv):
+         pay, buf_plane, buf_line, buf_pair, buf_chip,
+         load_sem, halo_send, halo_recv, sum_send, sum_recv):
     row = lax.axis_index("row")
     col = lax.axis_index("col")
     x_hi = row // PLANES
     z = row % PLANES
-    n_plane = (n_row // PLANES) * n_col
     place = x_hi * n_col + col
-
-    def plane_device(d):
-        return (row ^ ((d // n_col) * PLANES), col ^ (d % n_col))
-
-    def line_device(d):
-        return (row ^ d, col)
 
     ring = [[place_ for place_ in (at_, (at_ + 1) % size, (at_ + size - 1) % size)]
             for at_, size in ((row, n_row), (col, n_col))]
@@ -79,6 +68,7 @@
         return (ring[0][side[0]], ring[1][side[1]])
 
     loads = []
+    sends = []
     for n, (src, dst) in enumerate(((cen_h, cen_v), (rad_h, rad_v), (upp_h, upp_v), (obj_h, obj_v),
                                     (ker_h, ker_v), (low_h, low_v), (bia_h, bia_v))):
         copy = pltpu.make_async_copy(src, dst, load_sem.at[n])
@@ -87,11 +77,14 @@
 
     barrier = pltpu.get_barrier_semaphore()
     greeted = 0
-    for d in range(1, n_plane):
-        pl.semaphore_signal(barrier, inc=1, device_id=plane_device(d), device_id_type=MESH)
-        greeted += 1
-    for d in range(1, PLANES):
-        pl.semaphore_signal(barrier, inc=1, device_id=line_device(d), device_id_type=MESH)
+    for a in range(0, n_row, PLANES):
+        for b in range(n_col):
+            if a or b:
+                pl.semaphore_signal(barrier, inc=1, device_id=(row ^ a if a else row, col ^ b if b else col),
+                                    device_id_type=MESH)
+                greeted += 1
+    for a in range(1, PLANES):
+        pl.semaphore_signal(barrier, inc=1, device_id=(row ^ a, col), device_id_type=MESH)
         greeted += 1
     for side in SIDES:
         if side[0] != 0:
@@ -159,37 +152,60 @@
             dst_ref[first + top - deep : first + top, :] = cut(
                 jnp.logical_or(no_above, no_left), diag_dst[3, m])
 
-    sends = []
+    def far(d):
+        lines, across = d
+        z_, y_ = lines % PLANES, across // 4
+        return -(min(z_, PLANES - z_) + 2 * (lines // PLANES) + min(y_, 4 - y_) + (across % 4) // 2)
+
+    def order(row_steps, col_steps):
+        steps = [(a, b) for a in row_steps for b in col_steps if a or b]
+        return sorted(steps, key=far)
+
+    pair_steps = order((0,), (0, 1))
+    chip_steps = order(range(n_row), range(0, n_col, 2))
+    plane_steps = order(range(0, n_row, PLANES), range(n_col))
+    line_steps = order(range(PLANES), (0,))
+    chip = row * (n_col // 2) + col // 2
+
+    def stages(n):
+        if n == 0:
+            return ((plane_steps, buf_plane, place), (line_steps, buf_line, z))
+        return ((pair_steps, buf_pair.at[n - 1], col % 2), (chip_steps, buf_chip.at[n - 1], chip))
+
+    def exchange(n, stage, part):
+        steps, buf, slot = stages(n)[stage]
+        pay[n, stage] = part
+        buf[slot] = part
+        for a, b in steps:
+            pltpu.make_async_remote_copy(
+                src_ref=pay.at[n, stage], dst_ref=buf.at[slot],
+                send_sem=sum_send.at[n, stage], recv_sem=sum_recv.at[n, stage],
+                device_id=(row ^ a if a else row, col ^ b if b else col), device_id_type=MESH).start()
+
+    def whole(n, stage):
+        steps, buf, _ = stages(n)[stage]
+        part = buf.at[0 : len(steps)]
+        return pltpu.make_async_remote_copy(
+            src_ref=part, dst_ref=part, send_sem=sum_send.at[n, stage], recv_sem=sum_recv.at[n, stage],
+            device_id=side_device((0, 1)), device_id_type=MESH)
+
+    def collect(n, stage):
+        whole(n, stage).wait_recv()
+        return jnp.sum(stages(n)[stage][1][...], axis=0)
+
+    low_half = lax.broadcasted_iota(jnp.int32, (1, 128), 1) < CH
+
+    def fold(v):
+        return v + pltpu.roll(v, CH, 1)
 
     def sum_start(n, first_row, second_row):
-        pay_a[n, 0:1] = first_row
-        pay_a[n, 1:2] = second_row
-        buf_a[n, place, 0:1] = first_row
-        buf_a[n, place, 1:2] = second_row
-        for d in range(1, n_plane):
-            pltpu.make_async_remote_copy(
-                src_ref=pay_a.at[n], dst_ref=buf_a.at[n, place], send_sem=a_send.at[n], recv_sem=a_recv.at[n],
-                device_id=plane_device(d), device_id_type=MESH).start()
-
-    def whole(buf, n, count, send, recv):
-        part = buf.at[n, 0:count]
-        return pltpu.make_async_remote_copy(
-            src_ref=part, dst_ref=part, send_sem=send.at[n], recv_sem=recv.at[n],
-            device_id=side_device((0, 1)), device_id_type=MESH)
+        exchange(n, 0, jnp.where(low_half, fold(first_row), fold(second_row)))
 
     def sum_middle(n):
-        whole(buf_a, n, n_plane - 1, a_send, a_recv).wait_recv()
-        part = jnp.sum(buf_a[n], axis=0)
-        pay_b[n] = part
-        buf_b[n, z] = part
-        for d in range(1, PLANES):
-            pltpu.make_async_remote_copy(
-                src_ref=pay_b.at[n], dst_ref=buf_b.at[n, z], send_sem=b_send.at[n], recv_sem=b_recv.at[n],
-                device_id=line_device(d), device_id_type=MESH).start()
+        exchange(n, 1, collect(n, 0))
 
     def sum_end(n):
-        whole(buf_b, n, PLANES - 1, b_send, b_recv).wait_recv()
-        return jnp.sum(buf_b[n], axis=0)
+        return collect(n, 1)
 
     lane = lax.broadcasted_iota(jnp.int32, (EXT, 128), 1) < CH
     lane_w = lax.broadcasted_iota(jnp.int32, (WIDE, 128), 1) < CH
@@ -330,26 +346,31 @@
     halo_place(wide_in, 5, 1, EXT, 1, EPAIRS, bufs0)
 
     def value_terms(i, j):
-        q = -0.5
         total = base[inner(OBJ, j), :] * bias[DEPTH : DEPTH + 1]
-        mid, half = base[inner(MID, j), :], base[inner(HALF, j), :]
         hs = [base[inner(n, j), :] for n in (H1, H2, H3)]
-        qs = [base[inner(n, j), :] for n in (Q1, Q2, Q3)]
         t3 = tb[inner(0, j), :]
+        args = []
         if i == 0:
-            total += q * softplus(-4.0 * hs[2] * t3)
-            return total
-        g0 = g_x[ext_inner(0, j), :]
-        total += g0 * (mid - half) + q * softplus(-4.0 * half * g0)
-        lams = [lam_x[ext_inner(0, j), :], lam_x[ext_inner(1, j), :], lam[inner(0, j), :]]
-        mus = [mu_x[ext_inner(0, j), :], mu_x[ext_inner(1, j), :], mu[inner(0, j), :]]
-        for m in range(DEPTH):
-            g = g_x[ext_inner(m + 1, j), :] if m < 2 else mus[2] + t3
-            total += q * softplus(-4.0 * hs[m] * g)
-            total += q * softplus(-4.0 * hs[m] * (lams[m] - mus[m]))
-            total += q * softplus(4.0 * qs[m] * lams[m])
-            total -= lams[m] * bias[m : m + 1]
-        return total
+            args.append(-4.0 * hs[2] * t3)
+        else:
+            mid, half = base[inner(MID, j), :], base[inner(HALF, j), :]
+            qs = [base[inner(n, j), :] for n in (Q1, Q2, Q3)]
+            g0 = -trans[ext_inner(0, j), :]
+            total += g0 * (mid - half)
+            args.append(-4.0 * half * g0)
+            lams = [lam_x[ext_inner(0, j), :], lam_x[ext_inner(1, j), :], lam[inner(0, j), :]]
+            mus = [mu_x[ext_inner(0, j), :], mu_x[ext_inner(1, j), :], mu[inner(0, j), :]]
+            for m in range(DEPTH):
+                g = mus[m] - trans[ext_inner(m + 1, j), :] if m < 2 else mus[2] + t3
+                h4 = -4.0 * hs[m]
+                args += [h4 * g, h4 * (lams[m] - mus[m]), 4.0 * qs[m] * lams[m]]
+                total -= lams[m] * bias[m : m + 1]
+        product = 1.0 + jnp.exp(-jnp.abs(args[0]))
+        positive = jnp.maximum(args[0], 0.0)
+        for arg in args[1:]:
+            product = product * (1.0 + jnp.exp(-jnp.abs(arg)))
+            positive = positive + jnp.maximum(arg, 0.0)
+        return total - 0.5 * (positive + jnp.log(product))
 
     def value_row(i):
         def step(j, acc):
@@ -396,7 +417,6 @@
                             t = trans[ext(k, e), :] + t
                         trans[ext(k, e), :] = t
                         coef = -t if k == 0 else mus[k - 1][0] - t
-                        g_x[ext(k, e), :] = coef
                         xs.append(mids[k] - halfs[k] * jnp.tanh(2.0 * halfs[k] * coef))
                     for m in range(2):
                         h = halfs[m + 1]
@@ -471,7 +491,7 @@
         else:
             sum_middle(ITERS)
         both = sum_end(i)
-        squares = jnp.sum(both[0:1], axis=1, keepdims=True)
+        squares = jnp.sum(jnp.where(low_half, both, 0.0), axis=1, keepdims=True)
         scale = steps[i] / jnp.sqrt(squares / (2 * DEPTH * total_cells) + EPS)
         scale = jnp.broadcast_to(scale, (1, 128))
         totals.append(both)
@@ -487,14 +507,14 @@
     lax.fori_loop(0, PAIRS, finish, 0)
     totals.append(sum_end(ITERS))
     for i in range(ITERS):
-        mean = jnp.sum(totals[i + 1][1:2], axis=1, keepdims=True) / total_cells
+        mean = jnp.sum(jnp.where(low_half, 0.0, totals[i + 1]), axis=1, keepdims=True) / total_cells
         bounds_ref[i : i + 1, :] = jnp.broadcast_to(mean, (1, 128))
 
     for copy in sends:
         copy.wait_send()
     for n in range(ITERS + 1):
-        whole(buf_a, n, n_plane - 1, a_send, a_recv).wait_send()
-        whole(buf_b, n, PLANES - 1, b_send, b_recv).wait_send()
+        for stage in range(2):
+            whole(n, stage).wait_send()
 
 
 def store(bounds_v, lam_v, mu_v, bounds_out, lam_out, mu_out, sem):
@@ -542,7 +562,7 @@
                 vm(2 * ext_rows, 128), vm(2 * ext_rows, 128),
                 vm(3 * inner_rows, 128), vm(inner_rows, 128), vm(2 * ext_rows, 128),
                 vm(3 * ext_rows, 128), vm(3 * ext_rows, 128),
-                vm(3 * ext_rows, 128), vm(2 * ext_rows, 128),
+                vm(2 * ext_rows, 128),
                 vm(3 * inner_rows, 128), vm(inner_rows, 128),
                 vm(3 * (EPAIRS + 1) * WIDE, 128),
                 [vm(EXT, 128)] * 12, [vm(WIDE, 128)] * 9,
@@ -552,12 +572,11 @@
                 vm(2, 5, 1, PAIRS, 128), vm(2, 5, ROWS, 128), vm(4, 5, 1, 128),
                 vm(2, 2, 3, 2, PAIRS, 128), vm(2, 2, 3, ROWS, 128), vm(2, 4, 3, 2, 128),
                 vm(2, 2, 3, 2, PAIRS, 128), vm(2, 2, 3, ROWS, 128), vm(2, 4, 3, 2, 128),
-                vm(ITERS + 1, 2, 128), vm(ITERS + 1, n_plane, 2, 128),
-                vm(ITERS + 1, 2, 128), vm(ITERS + 1, PLANES, 2, 128),
+                vm(ITERS + 1, 2, 1, 128), vm(n_plane, 1, 128), vm(PLANES, 1, 128),
+                vm(ITERS, 2, 1, 128), vm(ITERS, n_row * n_col // 2, 1, 128),
                 pltpu.SemaphoreType.DMA((7,)),
                 pltpu.SemaphoreType.DMA((3, 8)), pltpu.SemaphoreType.DMA((3, 8)),
-                pltpu.SemaphoreType.DMA((ITERS + 1,)), pltpu.SemaphoreType.DMA((ITERS + 1,)),
-                pltpu.SemaphoreType.DMA((ITERS + 1,)), pltpu.SemaphoreType.DMA((ITERS + 1,)),
+                pltpu.SemaphoreType.DMA((ITERS + 1, 2)), pltpu.SemaphoreType.DMA((ITERS + 1, 2)),
             ],
             compiler_params=pltpu.CompilerParams(
                 collective_id=0, has_side_effects=True, vmem_limit_bytes=56 * 1024 * 1024),

time: 52.6 us -> 50.8 us (0.966)
  Pallas kernels: 51.8 us -> 50.1 us
    pallas_call x1, Pallas kernels: 50.4 us -> 48.7 us  [shards(): results = call(*args)]
where the time goes in v4:
time: 50.8 us; the launch traced here: 50.7 us
  Pallas kernels  50.1 us (99%)
  between operations  0.64 us (1%)
    pallas_call x1, Pallas kernels, shards(): results = call(*args)  48.7 us
    pallas_call x1, Pallas kernels, shards(): pl.pallas_call(store, out_shape=(jax.ShapeDtypeStruct((ITERS,), F32), jax...  1.41 us

profile of v4, /device:TPU:1, one launch (start us, length us, event | category | flops | bytes accessed | tf_op | source)
XLA Modules:
  0.0 50.7 jit_solution(14390777800205687405)
XLA Ops:
  0.6 48.7 %ascent.1 = (f32[8,128]{1,0:T(8,128)S(1)}, f32[3,16,2048]{2,1,0:T(8,128)S(1)}, f32[3,16,2048]{2,1,0:T(8,128)S(1)}) custom-call(f32[16,2048]{1,0:T(8,128)} %refs_0_.1, bf16[16,2048]{1,0:T(8,128)(2,1)} %refs_1_.1, bf16[16,2048]{1,0:T(8,128)(2,1)} %refs_2_.1, bf16[3,16,2048]{2,1,0:T(8,128)(2,1)} %refs_3_.1, bf16[3,16,2048]{2,1,0:T(8,128)(2,1)} %refs_4_.1, ...), custom_call_target="tpu_custom_call" | custom-call | tf_op jit(solution)/shard_map/ascent/pallas_call | solution.py:585
  49.3 1.4 %store.1 = (f32[3]{0:T(128)}, f32[3,16,2048]{2,1,0:T(8,128)}, f32[3,16,2048]{2,1,0:T(8,128)}) custom-call(f32[8,128]{1,0:T(8,128)S(1)} %get-tuple-element.6.bounds_v, f32[3,16,2048]{2,1,0:T(8,128)S(1)} %get-tuple-element.7.lam_v, f32[3,16,2048]{2,1,0:T(8,128)S(1)} %get-tuple-element.8.mu_v), custom_call_target="tpu_custom_call" | custom-call | tf_op jit(solution)/shard_map/store/pallas_call | solution.py:586

commit v5 on v4

--- a/solution.py
+++ b/solution.py
@@ -231,9 +231,42 @@
                 tiles.append(lhs_i[slot, part, dh, ROWS : size + ROWS, :])
                 tiles.append(lhs_i[slot, part, dh, 2 * ROWS : size + 2 * ROWS, :])
             halves.append(jnp.concatenate(tiles, axis=1))
-        high = jnp.dot(halves[0], wts[weight], preferred_element_type=F32)
-        low = jnp.dot(halves[1], wts[weight, :, 0:128], preferred_element_type=F32)
+        return product(halves[0], halves[1], weight)
+
+    def product(hi, lo, weight):
+        high = jnp.dot(hi, wts[weight], preferred_element_type=F32)
+        low = jnp.dot(lo, wts[weight, :, 0:128], preferred_element_type=F32)
         return (low + high[:, 128:]) + high[:, :128]
+
+    def rim(which, weight, scratch):
+        lane_r = lane[0:ROWS]
+        none = jnp.zeros((ROWS, 128), F32)
+        start = which * EPAIRS * EXT
+        sides = []
+        for s in (0, ROWS + 1):
+            x = [turn(wide_in[pl.ds(start + k * EXT + s, PAIRS, stride=EXT), :]) for k in range(3)]
+            sides.append([jnp.where(lane_r, x[0], x[1]), jnp.where(lane_r, x[1], x[2])])
+        left = jnp.where(lane_r, turn(wide_in[pl.ds(start + 1, ROWS), :]), none)
+        right = jnp.where(lane_r, none, turn(wide_in[pl.ds(start + (EPAIRS - 1) * EXT + 1, ROWS), :]))
+        for y, v in zip(scratch, (left, right)):
+            y[0:8, :] = zero_tile
+            y[16:24, :] = zero_tile
+            y[1 : ROWS + 1, :] = v
+        blocks = [sides[0] + [none] * 4, [none] * 4 + sides[1], [], []]
+        for dh in range(3):
+            blocks[2] += [scratch[0][dh : dh + ROWS, :], none]
+            blocks[3] += [none, scratch[1][dh : dh + ROWS, :]]
+        parts = [split(jnp.concatenate([b[k] for b in blocks], axis=0)) for k in range(6)]
+        return product(jnp.concatenate([p[0] for p in parts], axis=1),
+                       jnp.concatenate([p[1] for p in parts], axis=1), weight)
+
+    def add_rim(dst, first, v):
+        for at_, stride, k in ((0, ROWS, 0), (ROWS - 1, ROWS, 1)):
+            rows = pl.ds(first + at_, PAIRS, stride=stride)
+            dst[rows, :] = dst[rows, :] + v[k * ROWS : (k + 1) * ROWS]
+        for pair, k in ((0, 2), (PAIRS - 1, 3)):
+            rows = pl.ds(first + pair * ROWS, ROWS)
+            dst[rows, :] = dst[rows, :] + v[k * ROWS : (k + 1) * ROWS]
 
     def windows_wide():
         def wide(m, p):
@@ -340,10 +373,6 @@
         d_w[at(t * WIDE, WIDE), :] = jnp.zeros((WIDE, 128), F32)
         return carry
     lax.fori_loop(0, DEPTH * (EPAIRS + 1), clear, 0)
-
-    for copy in first_copies:
-        copy.wait_recv()
-    halo_place(wide_in, 5, 1, EXT, 1, EPAIRS, bufs0)
 
     def value_terms(i, j):
         total = base[inner(OBJ, j), :] * bias[DEPTH : DEPTH + 1]
@@ -433,19 +462,39 @@
 
         acc = jnp.zeros((ROWS, 128), F32)
         if i == 0:
-            back = conv(DEPTH, 3 + DEPTH)
+            for m in range(DEPTH):
+                image = conv(m, m)
+                for j in range(PAIRS):
+                    dl[inner(m, j), :] = image[j * ROWS : (j + 1) * ROWS]
+            image = conv(DEPTH, 3 + DEPTH)
             for j in range(PAIRS):
-                tb[inner(0, j), :] = back[j * ROWS : (j + 1) * ROWS]
-        for m in (2, 0, 1):
-            rest = []
+                tb[inner(0, j), :] = image[j * ROWS : (j + 1) * ROWS]
+            for copy in first_copies:
+                copy.wait_recv()
+            halo_place(wide_in, 5, 1, EXT, 1, EPAIRS, bufs0)
+            add_rim(tb, 0, rim(OBJ, 3 + DEPTH, y_s[0:2]))
+            for m in range(DEPTH):
+                add_rim(dl, m * PAIRS * ROWS, rim((MID, H1, H2)[m], m, y_s[2 * m + 2 : 2 * m + 4]))
             for j in range(PAIRS):
-                h = base[inner(H1 + m if m < 2 else H3, j), :]
-                q = base[inner(Q1 + m, j), :]
-                if m == 2:
-                    t3 = tb[inner(0, j), :]
-                    if i == 0:
-                        p, v_lam = h, None
+                for m in range(DEPTH):
+                    h = base[inner(H1 + m if m < 2 else H3, j), :]
+                    p = h if m == 2 else p_x[ext_inner(m, j), :]
+                    if m == 2:
+                        v = (h - h * jnp.tanh(2.0 * h * tb[inner(0, j), :])) - p
+                        dmu[inner(0, j), :] = v
                     else:
+                        v = dmu_x[ext_inner(m, j), :]
+                    acc = acc + v * v
+                    v = (p - base[inner(Q1 + m, j), :] - bias[m : m + 1]) - dl[inner(m, j), :]
+                    dl[inner(m, j), :] = v
+                    d_w[pl.ds((m * (EPAIRS + 1) + j + 1) * WIDE + 2, ROWS), :] = v
+                    acc = acc + v * v
+        else:
+            for m in (2, 0, 1):
+                for j in range(PAIRS):
+                    h = base[inner(H1 + m if m < 2 else H3, j), :]
+                    q = base[inner(Q1 + m, j), :]
+                    if m == 2:
                         new_mu = scale * dmu[inner(0, j), :]
                         v_lam = scale * dl[inner(2, j), :]
                         if not first:
@@ -454,22 +503,22 @@
                         mu[inner(0, j), :] = new_mu
                         lam[inner(0, j), :] = v_lam
                         p = h - h * jnp.tanh(2.0 * h * (v_lam - new_mu))
-                        t3 = new_mu + t3
-                    v = (h - h * jnp.tanh(2.0 * h * t3)) - p
-                    dmu[inner(0, j), :] = v
-                else:
-                    p = p_x[ext_inner(m, j), :]
-                    v_lam = None if i == 0 else lam_x[ext_inner(m, j), :]
-                    v = dmu_x[ext_inner(m, j), :]
-                acc = acc + v * v
-                n = q if i == 0 else q + q * jnp.tanh(2.0 * q * v_lam)
-                pn[inner(m, j), :] = p - n - bias[m : m + 1]
-            image = conv(m, m)
-            for j in range(PAIRS):
-                v = pn[inner(m, j), :] - image[j * ROWS : (j + 1) * ROWS]
-                dl[inner(m, j), :] = v
-                d_w[pl.ds((m * (EPAIRS + 1) + j + 1) * WIDE + 2, ROWS), :] = v
-                acc = acc + v * v
+                        t3 = new_mu + tb[inner(0, j), :]
+                        v = (h - h * jnp.tanh(2.0 * h * t3)) - p
+                        dmu[inner(0, j), :] = v
+                    else:
+                        p = p_x[ext_inner(m, j), :]
+                        v_lam = lam_x[ext_inner(m, j), :]
+                        v = dmu_x[ext_inner(m, j), :]
+                    acc = acc + v * v
+                    n = q + q * jnp.tanh(2.0 * q * v_lam)
+                    pn[inner(m, j), :] = p - n - bias[m : m + 1]
+                image = conv(m, m)
+                for j in range(PAIRS):
+                    v = pn[inner(m, j), :] - image[j * ROWS : (j + 1) * ROWS]
+                    dl[inner(m, j), :] = v
+                    d_w[pl.ds((m * (EPAIRS + 1) + j + 1) * WIDE + 2, ROWS), :] = v
+                    acc = acc + v * v
         sum_start(i, jnp.sum(acc, axis=0, keepdims=True), value_prev)
 
         copies = []

time: 50.8 us -> 49.8 us (0.980)
  Pallas kernels: 50.1 us -> 49 us
    pallas_call x1, Pallas kernels: 48.7 us -> 47.6 us  [shards(): results = call(*args)]
where the time goes in v5:
time: 49.8 us; the launch traced here: 49.7 us
  Pallas kernels  49 us (98%)
  between operations  0.64 us (1%)
    pallas_call x1, Pallas kernels, shards(): results = call(*args)  47.6 us
    pallas_call x1, Pallas kernels, shards(): pl.pallas_call(store, out_shape=(jax.ShapeDtypeStruct((ITERS,), F32), jax...  1.41 us

profile of v5, /device:TPU:1, one launch (start us, length us, event | category | flops | bytes accessed | tf_op | source)
XLA Modules:
  0.0 49.7 jit_solution(11070445135828001527)
XLA Ops:
  0.6 47.6 %ascent.1 = (f32[8,128]{1,0:T(8,128)S(1)}, f32[3,16,2048]{2,1,0:T(8,128)S(1)}, f32[3,16,2048]{2,1,0:T(8,128)S(1)}) custom-call(f32[16,2048]{1,0:T(8,128)} %refs_0_.1, bf16[16,2048]{1,0:T(8,128)(2,1)} %refs_1_.1, bf16[16,2048]{1,0:T(8,128)(2,1)} %refs_2_.1, bf16[3,16,2048]{2,1,0:T(8,128)(2,1)} %refs_3_.1, bf16[3,16,2048]{2,1,0:T(8,128)(2,1)} %refs_4_.1, ...), custom_call_target="tpu_custom_call" | custom-call | tf_op jit(solution)/shard_map/ascent/pallas_call | solution.py:634
  48.3 1.4 %store.1 = (f32[3]{0:T(128)}, f32[3,16,2048]{2,1,0:T(8,128)}, f32[3,16,2048]{2,1,0:T(8,128)}) custom-call(f32[8,128]{1,0:T(8,128)S(1)} %get-tuple-element.6.bounds_v, f32[3,16,2048]{2,1,0:T(8,128)S(1)} %get-tuple-element.7.lam_v, f32[3,16,2048]{2,1,0:T(8,128)S(1)} %get-tuple-element.8.mu_v), custom_call_target="tpu_custom_call" | custom-call | tf_op jit(solution)/shard_map/store/pallas_call | solution.py:635

commit v6 on v5

--- a/solution.py
+++ b/solution.py
@@ -19,6 +19,7 @@
 EXT = 24
 EPAIRS = 18
 WIDE = 32
+TOP = 8
 PLANES = 8
 MID, HALF, H1, H2, OBJ, H3, Q1, Q2, Q3 = range(9)
 UP, DOWN, LEFT, RIGHT = range(4)
@@ -31,6 +32,10 @@
 
 def inner(which, pair):
     return at((which * PAIRS + pair) * ROWS, ROWS)
+
+
+def slope(which, pair):
+    return at((which * (EPAIRS + 1) + pair + 1) * WIDE + TOP, ROWS)
 
 
 def ext(which, pair):
@@ -77,6 +82,10 @@
 
     barrier = pltpu.get_barrier_semaphore()
     greeted = 0
+    for side in SIDES:
+        if side[0] != 0:
+            pl.semaphore_signal(barrier, inc=1, device_id=side_device(side), device_id_type=MESH)
+            greeted += 1
     for a in range(0, n_row, PLANES):
         for b in range(n_col):
             if a or b:
@@ -86,27 +95,21 @@
     for a in range(1, PLANES):
         pl.semaphore_signal(barrier, inc=1, device_id=(row ^ a, col), device_id_type=MESH)
         greeted += 1
-    for side in SIDES:
-        if side[0] != 0:
-            pl.semaphore_signal(barrier, inc=1, device_id=side_device(side), device_id_type=MESH)
-            greeted += 1
 
     zero_tile = jnp.zeros((8, 128), F32)
 
-    def halo_start(n, src_ref, maps, deep, bufs):
+    def halo_start(n, src_ref, start, step, tall, maps, deep, bufs):
         rows_src, cols_src, diag_src, rows_dst, cols_dst, diag_dst = bufs
         for m in range(maps):
-            first = m * PAIRS * ROWS
+            first = start + m * step
+            last = first + (PAIRS - 1) * tall
             for r in range(deep):
-                rows_src[UP, m, r] = src_ref[pl.ds(first + r, PAIRS, stride=ROWS), :]
-                rows_src[DOWN, m, r] = src_ref[pl.ds(first + ROWS - deep + r, PAIRS, stride=ROWS), :]
-            cols_src[0, m] = src_ref[first : first + ROWS, :]
-            cols_src[1, m] = src_ref[first + (PAIRS - 1) * ROWS : first + PAIRS * ROWS, :]
-            last = first + (PAIRS - 1) * ROWS
-            diag_src[0, m] = src_ref[first : first + deep, :]
-            diag_src[1, m] = src_ref[last : last + deep, :]
-            diag_src[2, m] = src_ref[first + ROWS - deep : first + ROWS, :]
-            diag_src[3, m] = src_ref[last + ROWS - deep : last + ROWS, :]
+                rows_src[UP, m, r] = src_ref[pl.ds(first + r, PAIRS, stride=tall), :]
+                rows_src[DOWN, m, r] = src_ref[pl.ds(first + ROWS - deep + r, PAIRS, stride=tall), :]
+            for side, at_ in ((0, first), (1, last)):
+                cols_src[side, m] = src_ref[at_ : at_ + ROWS, :]
+                diag_src[side, m] = src_ref[at_ : at_ + deep, :]
+                diag_src[side + 2, m] = src_ref[at_ + ROWS - deep : at_ + ROWS, :]
         copies = []
         for s in (4, 5, 6, 7, 0, 1, 2, 3):
             if s < 2:
@@ -288,7 +291,7 @@
                 for i, y in enumerate((ya, yb, yc)):
                     y_w[m * 3 + i][...] = y
                 for dh in range(3):
-                    ys = [y_w[m * 3 + i][dh : dh + EXT, :] for i in range(3)]
+                    ys = [y_w[m * 3 + i][dh + TOP - 2 : dh + TOP - 2 + EXT, :] for i in range(3)]
                     for half in range(2):
                         hi, lo = split(jnp.concatenate([ys[half], ys[half + 1]], axis=0))
                         rows = pl.ds(pl.multiple_of(t * 2 * EXT, 16), 2 * EXT)
@@ -329,7 +332,7 @@
 
     pl.semaphore_wait(barrier, greeted)
     bufs0 = (rows_s0, cols_s0, diag_s0, rows_r0, cols_r0, diag_r0)
-    first_copies = halo_start(0, base, 5, 1, bufs0)
+    first_copies = halo_start(0, base, 0, PAIRS * ROWS, ROWS, 5, 1, bufs0)
     sends += first_copies
 
     for n in range(4, 7):
@@ -416,49 +419,55 @@
     for i in range(ITERS):
         first = i == 1
 
-        def step_x(g, carry):
+        def start_x(g, carry):
             before = list(carry)
             for u in range(3):
                 e = 3 * g + u
-                if i == 0:
-                    xs = [wide_in[ext(n, e), :] for n in (MID, H1, H2)]
-                    for m in range(2):
-                        p_x[ext(m, e), :] = xs[m + 1]
-                        dmu_x[ext(m, e), :] = xs[m + 1] - p_x[ext(m, e), :]
-                    xs.append(wide_in[ext(OBJ, e), :])
-                else:
-                    halfs = [wide_in[ext(n, e), :] for n in (HALF, H1, H2)]
-                    mids = [wide_in[ext(MID, e), :], halfs[1], halfs[2]]
-                    xs = []
-                    mus = []
-                    for m in range(2):
-                        new_mu = scale * dmu_x[ext(m, e), :]
-                        new_lam = scale * d_w[pl.ds((m * (EPAIRS + 1) + e) * WIDE + 1, EXT), :]
-                        if not first:
-                            new_mu = mu_x[ext(m, e), :] + new_mu
-                            new_lam = lam_x[ext(m, e), :] + new_lam
-                        mu_x[ext(m, e), :] = new_mu
-                        lam_x[ext(m, e), :] = new_lam
-                        mus.append((new_mu, new_lam))
-                    for k in range(DEPTH):
-                        t = scale * upd[ext(k, e), :]
-                        if not first:
-                            t = trans[ext(k, e), :] + t
-                        trans[ext(k, e), :] = t
-                        coef = -t if k == 0 else mus[k - 1][0] - t
-                        xs.append(mids[k] - halfs[k] * jnp.tanh(2.0 * halfs[k] * coef))
-                    for m in range(2):
-                        h = halfs[m + 1]
-                        p = h - h * jnp.tanh(2.0 * h * (mus[m][1] - mus[m][0]))
-                        p_x[ext(m, e), :] = p
-                        dmu_x[ext(m, e), :] = xs[m + 1] - p
+                xs = [wide_in[ext(n, e), :] for n in (MID, H1, H2)]
+                for m in range(2):
+                    p_x[ext(m, e), :] = xs[m + 1]
+                    dmu_x[ext(m, e), :] = xs[m + 1] - p_x[ext(m, e), :]
+                xs.append(wide_in[ext(OBJ, e), :])
                 for k, x in enumerate(xs):
                     now = turn(x)
                     window(k, u, e, before[k], now)
                     before[k] = now
             return tuple(before)
-        maps = LAYERS if i == 0 else DEPTH
-        lax.fori_loop(0, EPAIRS // 3, step_x, tuple(jnp.zeros((EXT, 128), F32) for _ in range(maps)))
+
+        def step_x(k):
+            before = jnp.zeros((EXT, 128), F32)
+            for e in range(EPAIRS):
+                half = wide_in[ext((HALF, H1, H2)[k], e), :]
+                mid = wide_in[ext(MID, e), :] if k == 0 else half
+                t = scale * upd[ext(k, e), :]
+                if not first:
+                    t = trans[ext(k, e), :] + t
+                trans[ext(k, e), :] = t
+                coef = -t
+                if k > 0:
+                    m = k - 1
+                    new_mu = scale * dmu_x[ext(m, e), :]
+                    new_lam = scale * d_w[pl.ds((m * (EPAIRS + 1) + e) * WIDE + TOP - 1, EXT), :]
+                    if not first:
+                        new_mu = mu_x[ext(m, e), :] + new_mu
+                        new_lam = lam_x[ext(m, e), :] + new_lam
+                    mu_x[ext(m, e), :] = new_mu
+                    lam_x[ext(m, e), :] = new_lam
+                    coef = new_mu - t
+                x = mid - half * jnp.tanh(2.0 * half * coef)
+                if k > 0:
+                    p = half - half * jnp.tanh(2.0 * half * (new_lam - new_mu))
+                    p_x[ext(m, e), :] = p
+                    dmu_x[ext(m, e), :] = x - p
+                now = turn(x)
+                window(k, e % 3, e, before, now)
+                before = now
+
+        if i == 0:
+            lax.fori_loop(0, EPAIRS // 3, start_x, tuple(jnp.zeros((EXT, 128), F32) for _ in range(LAYERS)))
+        else:
+            step_x(0)
+            step_x(1)
 
         acc = jnp.zeros((ROWS, 128), F32)
         if i == 0:
@@ -486,17 +495,17 @@
                         v = dmu_x[ext_inner(m, j), :]
                     acc = acc + v * v
                     v = (p - base[inner(Q1 + m, j), :] - bias[m : m + 1]) - dl[inner(m, j), :]
-                    dl[inner(m, j), :] = v
-                    d_w[pl.ds((m * (EPAIRS + 1) + j + 1) * WIDE + 2, ROWS), :] = v
+                    d_w[slope(m, j), :] = v
                     acc = acc + v * v
         else:
-            for m in (2, 0, 1):
+            for m in range(DEPTH):
+                rest = []
                 for j in range(PAIRS):
                     h = base[inner(H1 + m if m < 2 else H3, j), :]
                     q = base[inner(Q1 + m, j), :]
                     if m == 2:
                         new_mu = scale * dmu[inner(0, j), :]
-                        v_lam = scale * dl[inner(2, j), :]
+                        v_lam = scale * d_w[slope(2, j), :]
                         if not first:
                             new_mu = mu[inner(0, j), :] + new_mu
                             v_lam = lam[inner(0, j), :] + v_lam
@@ -512,19 +521,20 @@
                         v = dmu_x[ext_inner(m, j), :]
                     acc = acc + v * v
                     n = q + q * jnp.tanh(2.0 * q * v_lam)
-                    pn[inner(m, j), :] = p - n - bias[m : m + 1]
+                    rest.append(p - n - bias[m : m + 1])
                 image = conv(m, m)
                 for j in range(PAIRS):
-                    v = pn[inner(m, j), :] - image[j * ROWS : (j + 1) * ROWS]
-                    dl[inner(m, j), :] = v
-                    d_w[pl.ds((m * (EPAIRS + 1) + j + 1) * WIDE + 2, ROWS), :] = v
+                    v = rest[j] - image[j * ROWS : (j + 1) * ROWS]
+                    d_w[slope(m, j), :] = v
                     acc = acc + v * v
+                if m == 0:
+                    step_x(2)
         sum_start(i, jnp.sum(acc, axis=0, keepdims=True), value_prev)
 
         copies = []
         if i < ITERS - 1:
             bufs = tuple(ref.at[i] for ref in (rows_s, cols_s, diag_s, rows_r, cols_r, diag_r))
-            copies = halo_start(1 + i, dl, DEPTH, 2, bufs)
+            copies = halo_start(1 + i, d_w, WIDE + TOP, (EPAIRS + 1) * WIDE, WIDE, DEPTH, 2, bufs)
             sends += copies
         value_prev = value_row(i)
         if i == ITERS - 1:
@@ -533,7 +543,7 @@
         if i < ITERS - 1:
             for copy in copies:
                 copy.wait_recv()
-            halo_place(d_w, DEPTH, 2, WIDE, 2, EPAIRS + 1, bufs)
+            halo_place(d_w, DEPTH, 2, WIDE, TOP, EPAIRS + 1, bufs)
             windows_wide()
             for m in range(DEPTH):
                 conv_wide(m)
@@ -548,22 +558,22 @@
     def finish(j, carry):
         lanes = pl.ds(pl.multiple_of(j * 128, 128), 128)
         for m in range(2):
-            lam_out[m, :, lanes] = lam_x[ext_inner(m, j), :] + scale * dl[inner(m, j), :]
+            lam_out[m, :, lanes] = lam_x[ext_inner(m, j), :] + scale * d_w[slope(m, j), :]
             mu_out[m, :, lanes] = mu_x[ext_inner(m, j), :] + scale * dmu_x[ext_inner(m, j), :]
-        lam_out[2, :, lanes] = lam[inner(0, j), :] + scale * dl[inner(2, j), :]
+        lam_out[2, :, lanes] = lam[inner(0, j), :] + scale * d_w[slope(2, j), :]
         mu_out[2, :, lanes] = mu[inner(0, j), :] + scale * dmu[inner(0, j), :]
         return carry
     lax.fori_loop(0, PAIRS, finish, 0)
-    totals.append(sum_end(ITERS))
-    for i in range(ITERS):
-        mean = jnp.sum(jnp.where(low_half, 0.0, totals[i + 1]), axis=1, keepdims=True) / total_cells
-        bounds_ref[i : i + 1, :] = jnp.broadcast_to(mean, (1, 128))
-
     for copy in sends:
         copy.wait_send()
     for n in range(ITERS + 1):
         for stage in range(2):
             whole(n, stage).wait_send()
+    for i in range(ITERS):
+        if i == ITERS - 1:
+            totals.append(sum_end(ITERS))
+        mean = jnp.sum(jnp.where(low_half, 0.0, totals[i + 1]), axis=1, keepdims=True) / total_cells
+        bounds_ref[i : i + 1, :] = jnp.broadcast_to(mean, (1, 128))
 
 
 def store(bounds_v, lam_v, mu_v, bounds_out, lam_out, mu_out, sem):

time: 49.8 us -> 48.8 us (0.980)
  Pallas kernels: 49 us -> 48.1 us
    pallas_call x1, Pallas kernels: 47.6 us -> 46.7 us  [shards(): results = call(*args)]
where the time goes in v6:
time: 48.8 us; the launch traced here: 48.7 us
  Pallas kernels  48.1 us (99%)
  between operations  0.64 us (1%)
    pallas_call x1, Pallas kernels, shards(): results = call(*args)  46.7 us
    pallas_call x1, Pallas kernels, shards(): pl.pallas_call(store, out_shape=(jax.ShapeDtypeStruct((ITERS,), F32), jax...  1.41 us

profile of v6, /device:TPU:1, one launch (start us, length us, event | category | flops | bytes accessed | tf_op | source)
XLA Modules:
  0.0 48.7 jit_solution(6490996487574125561)
XLA Ops:
  0.6 46.7 %ascent.1 = (f32[8,128]{1,0:T(8,128)S(1)}, f32[3,16,2048]{2,1,0:T(8,128)S(1)}, f32[3,16,2048]{2,1,0:T(8,128)S(1)}) custom-call(f32[16,2048]{1,0:T(8,128)} %refs_0_.1, bf16[16,2048]{1,0:T(8,128)(2,1)} %refs_1_.1, bf16[16,2048]{1,0:T(8,128)(2,1)} %refs_2_.1, bf16[3,16,2048]{2,1,0:T(8,128)(2,1)} %refs_3_.1, bf16[3,16,2048]{2,1,0:T(8,128)(2,1)} %refs_4_.1, ...), custom_call_target="tpu_custom_call" | custom-call | tf_op jit(solution)/shard_map/ascent/pallas_call | solution.py:644
  47.3 1.4 %store.1 = (f32[3]{0:T(128)}, f32[3,16,2048]{2,1,0:T(8,128)}, f32[3,16,2048]{2,1,0:T(8,128)}) custom-call(f32[8,128]{1,0:T(8,128)S(1)} %get-tuple-element.6.bounds_v, f32[3,16,2048]{2,1,0:T(8,128)S(1)} %get-tuple-element.7.lam_v, f32[3,16,2048]{2,1,0:T(8,128)S(1)} %get-tuple-element.8.mu_v), custom_call_target="tpu_custom_call" | custom-call | tf_op jit(solution)/shard_map/store/pallas_call | solution.py:645

commit v7 on v6

--- a/solution.py
+++ b/solution.py
@@ -44,6 +44,15 @@
 
 def ext_inner(which, pair):
     return pl.ds((which * EPAIRS + pair + 1) * EXT + 1, ROWS)
+
+
+def softplus_sum(args):
+    product = 1.0 + jnp.exp(-jnp.abs(args[0]))
+    positive = jnp.maximum(args[0], 0.0)
+    for arg in args[1:]:
+        product = product * (1.0 + jnp.exp(-jnp.abs(arg)))
+        positive = positive + jnp.maximum(arg, 0.0)
+    return positive + jnp.log(product)
 
 
 def split(v):
@@ -196,13 +205,19 @@
         whole(n, stage).wait_recv()
         return jnp.sum(stages(n)[stage][1][...], axis=0)
 
-    low_half = lax.broadcasted_iota(jnp.int32, (1, 128), 1) < CH
-
-    def fold(v):
-        return v + pltpu.roll(v, CH, 1)
-
-    def sum_start(n, first_row, second_row):
-        exchange(n, 0, jnp.where(low_half, fold(first_row), fold(second_row)))
+    lane_1 = lax.broadcasted_iota(jnp.int32, (1, 128), 1)
+    holds = (lane_1 < 32, jnp.logical_and(lane_1 >= 32, lane_1 < CH), lane_1 >= CH)
+
+    def fold_to(v, width):
+        step = CH
+        while step >= width:
+            v = v + pltpu.roll(v, step, 1)
+            step //= 2
+        return v
+
+    def sum_start(n, first_row, second_row, third_row):
+        exchange(n, 0, jnp.where(holds[0], fold_to(first_row, 32),
+                                 jnp.where(holds[1], fold_to(second_row, 32), fold_to(third_row, CH))))
 
     def sum_middle(n):
         exchange(n, 1, collect(n, 0))
@@ -325,7 +340,7 @@
                 wide_in[at((name * EPAIRS + j + 1) * EXT + 16, 8), :] = zero_tile
                 wide_in[ext_inner(name, j), :] = v
         return carry
-    lax.fori_loop(0, PAIRS, fill, 0)
+    lax.fori_loop(0, PAIRS, fill, 0, unroll=4)
     for m in range(5):
         for e in (0, EPAIRS - 1):
             wide_in[ext(m, e), :] = jnp.zeros((EXT, 128), F32)
@@ -397,12 +412,7 @@
                 h4 = -4.0 * hs[m]
                 args += [h4 * g, h4 * (lams[m] - mus[m]), 4.0 * qs[m] * lams[m]]
                 total -= lams[m] * bias[m : m + 1]
-        product = 1.0 + jnp.exp(-jnp.abs(args[0]))
-        positive = jnp.maximum(args[0], 0.0)
-        for arg in args[1:]:
-            product = product * (1.0 + jnp.exp(-jnp.abs(arg)))
-            positive = positive + jnp.maximum(arg, 0.0)
-        return total - 0.5 * (positive + jnp.log(product))
+        return total - 0.5 * softplus_sum(args)
 
     def value_row(i):
         def step(j, acc):
@@ -468,8 +478,11 @@
         else:
             step_x(0)
             step_x(1)
+            if i == ITERS - 1:
+                step_x(2)
 
         acc = jnp.zeros((ROWS, 128), F32)
+        value_last = jnp.zeros((ROWS, 128), F32)
         if i == 0:
             for m in range(DEPTH):
                 image = conv(m, m)
@@ -520,6 +533,21 @@
                         v_lam = lam_x[ext_inner(m, j), :]
                         v = dmu_x[ext_inner(m, j), :]
                     acc = acc + v * v
+                    if i == ITERS - 1:
+                        if m == 2:
+                            v_mu, coef = new_mu, t3
+                        else:
+                            v_mu = mu_x[ext_inner(m, j), :]
+                            coef = v_mu - trans[ext_inner(m + 1, j), :]
+                        args = [-4.0 * h * coef, -4.0 * h * (v_lam - v_mu), 4.0 * q * v_lam]
+                        part = -v_lam * bias[m : m + 1]
+                        if m == 0:
+                            half = base[inner(HALF, j), :]
+                            coef = -trans[ext_inner(0, j), :]
+                            args.append(-4.0 * half * coef)
+                            part += coef * (base[inner(MID, j), :] - half)
+                            part += base[inner(OBJ, j), :] * bias[DEPTH : DEPTH + 1]
+                        value_last = value_last + (part - 0.5 * softplus_sum(args))
                     n = q + q * jnp.tanh(2.0 * q * v_lam)
                     rest.append(p - n - bias[m : m + 1])
                 image = conv(m, m)
@@ -527,18 +555,17 @@
                     v = rest[j] - image[j * ROWS : (j + 1) * ROWS]
                     d_w[slope(m, j), :] = v
                     acc = acc + v * v
-                if m == 0:
+                if m == 0 and i < ITERS - 1:
                     step_x(2)
-        sum_start(i, jnp.sum(acc, axis=0, keepdims=True), value_prev)
+        sum_start(i, *[jnp.sum(v, axis=0, keepdims=True) for v in (acc, value_last)], value_prev)
 
         copies = []
         if i < ITERS - 1:
             bufs = tuple(ref.at[i] for ref in (rows_s, cols_s, diag_s, rows_r, cols_r, diag_r))
             copies = halo_start(1 + i, d_w, WIDE + TOP, (EPAIRS + 1) * WIDE, WIDE, DEPTH, 2, bufs)
             sends += copies
-        value_prev = value_row(i)
-        if i == ITERS - 1:
-            sum_start(ITERS, jnp.zeros((1, 128), F32), value_prev)
+        if i < ITERS - 1:
+            value_prev = value_row(i)
         sum_middle(i)
         if i < ITERS - 1:
             for copy in copies:
@@ -547,33 +574,29 @@
             windows_wide()
             for m in range(DEPTH):
                 conv_wide(m)
-        else:
-            sum_middle(ITERS)
+        if i == ITERS - 1:
+            for copy in sends:
+                copy.wait_send()
+            for n in range(ITERS):
+                for stage in range(2):
+                    whole(n, stage).wait_send()
         both = sum_end(i)
-        squares = jnp.sum(jnp.where(low_half, both, 0.0), axis=1, keepdims=True)
+        squares = jnp.sum(jnp.where(holds[0], both, 0.0), axis=1, keepdims=True)
         scale = steps[i] / jnp.sqrt(squares / (2 * DEPTH * total_cells) + EPS)
         scale = jnp.broadcast_to(scale, (1, 128))
         totals.append(both)
 
-    def finish(j, carry):
-        lanes = pl.ds(pl.multiple_of(j * 128, 128), 128)
+    for j in range(PAIRS):
+        lanes = pl.ds(j * 128, 128)
         for m in range(2):
             lam_out[m, :, lanes] = lam_x[ext_inner(m, j), :] + scale * d_w[slope(m, j), :]
             mu_out[m, :, lanes] = mu_x[ext_inner(m, j), :] + scale * dmu_x[ext_inner(m, j), :]
         lam_out[2, :, lanes] = lam[inner(0, j), :] + scale * d_w[slope(2, j), :]
         mu_out[2, :, lanes] = mu[inner(0, j), :] + scale * dmu[inner(0, j), :]
-        return carry
-    lax.fori_loop(0, PAIRS, finish, 0)
-    for copy in sends:
-        copy.wait_send()
-    for n in range(ITERS + 1):
-        for stage in range(2):
-            whole(n, stage).wait_send()
     for i in range(ITERS):
-        if i == ITERS - 1:
-            totals.append(sum_end(ITERS))
-        mean = jnp.sum(jnp.where(low_half, 0.0, totals[i + 1]), axis=1, keepdims=True) / total_cells
-        bounds_ref[i : i + 1, :] = jnp.broadcast_to(mean, (1, 128))
+        last = i == ITERS - 1
+        mean = jnp.sum(jnp.where(holds[1 if last else 2], totals[i if last else i + 1], 0.0), axis=1, keepdims=True)
+        bounds_ref[i : i + 1, :] = jnp.broadcast_to(mean / total_cells, (1, 128))
 
 
 def store(bounds_v, lam_v, mu_v, bounds_out, lam_out, mu_out, sem):
@@ -631,11 +654,11 @@
                 vm(2, 5, 1, PAIRS, 128), vm(2, 5, ROWS, 128), vm(4, 5, 1, 128),
                 vm(2, 2, 3, 2, PAIRS, 128), vm(2, 2, 3, ROWS, 128), vm(2, 4, 3, 2, 128),
                 vm(2, 2, 3, 2, PAIRS, 128), vm(2, 2, 3, ROWS, 128), vm(2, 4, 3, 2, 128),
-                vm(ITERS + 1, 2, 1, 128), vm(n_plane, 1, 128), vm(PLANES, 1, 128),
-                vm(ITERS, 2, 1, 128), vm(ITERS, n_row * n_col // 2, 1, 128),
+                vm(ITERS, 2, 1, 128), vm(n_plane, 1, 128), vm(PLANES, 1, 128),
+                vm(ITERS - 1, 2, 1, 128), vm(ITERS - 1, n_row * n_col // 2, 1, 128),
                 pltpu.SemaphoreType.DMA((7,)),
                 pltpu.SemaphoreType.DMA((3, 8)), pltpu.SemaphoreType.DMA((3, 8)),
-                pltpu.SemaphoreType.DMA((ITERS + 1, 2)), pltpu.SemaphoreType.DMA((ITERS + 1, 2)),
+                pltpu.SemaphoreType.DMA((ITERS, 2)), pltpu.SemaphoreType.DMA((ITERS, 2)),
             ],
             compiler_params=pltpu.CompilerParams(
                 collective_id=0, has_side_effects=True, vmem_limit_bytes=56 * 1024 * 1024),

time: 48.8 us -> 48.5 us (level)
  no operation moved by 1% of the time
where the time goes in v7:
time: 48.5 us; the launch traced here: 48.4 us
  Pallas kernels  47.7 us (98%)
  between operations  0.64 us (1%)
    pallas_call x1, Pallas kernels, shards(): results = call(*args)  46.3 us
    pallas_call x1, Pallas kernels, shards(): pl.pallas_call(store, out_shape=(jax.ShapeDtypeStruct((ITERS,), F32), jax...  1.41 us

profile of v7, /device:TPU:1, one launch (start us, length us, event | category | flops | bytes accessed | tf_op | source)
XLA Modules:
  0.0 48.4 jit_solution(3119262102603284453)
XLA Ops:
  0.6 46.3 %ascent.1 = (f32[8,128]{1,0:T(8,128)S(1)}, f32[3,16,2048]{2,1,0:T(8,128)S(1)}, f32[3,16,2048]{2,1,0:T(8,128)S(1)}) custom-call(f32[16,2048]{1,0:T(8,128)} %refs_0_.1, bf16[16,2048]{1,0:T(8,128)(2,1)} %refs_1_.1, bf16[16,2048]{1,0:T(8,128)(2,1)} %refs_2_.1, bf16[3,16,2048]{2,1,0:T(8,128)(2,1)} %refs_3_.1, bf16[3,16,2048]{2,1,0:T(8,128)(2,1)} %refs_4_.1, ...), custom_call_target="tpu_custom_call" | custom-call | tf_op jit(solution)/shard_map/ascent/pallas_call | solution.py:667
  46.9 1.4 %store.1 = (f32[3]{0:T(128)}, f32[3,16,2048]{2,1,0:T(8,128)}, f32[3,16,2048]{2,1,0:T(8,128)}) custom-call(f32[8,128]{1,0:T(8,128)S(1)} %get-tuple-element.6.bounds_v, f32[3,16,2048]{2,1,0:T(8,128)S(1)} %get-tuple-element.7.lam_v, f32[3,16,2048]{2,1,0:T(8,128)S(1)} %get-tuple-element.8.mu_v), custom_call_target="tpu_custom_call" | custom-call | tf_op jit(solution)/shard_map/store/pallas_call | solution.py:668

commit v8 on v7

--- a/solution.py
+++ b/solution.py
@@ -564,9 +564,11 @@
             bufs = tuple(ref.at[i] for ref in (rows_s, cols_s, diag_s, rows_r, cols_r, diag_r))
             copies = halo_start(1 + i, d_w, WIDE + TOP, (EPAIRS + 1) * WIDE, WIDE, DEPTH, 2, bufs)
             sends += copies
-        if i < ITERS - 1:
+        if i == 0:
             value_prev = value_row(i)
         sum_middle(i)
+        if 0 < i < ITERS - 1:
+            value_prev = value_row(i)
         if i < ITERS - 1:
             for copy in copies:
                 copy.wait_recv()

time: 48.5 us -> 48.5 us (level)
  no operation moved by 1% of the time
where the time goes in v8:
time: 48.5 us; the launch traced here: 48.4 us
  Pallas kernels  47.7 us (98%)
  between operations  0.64 us (1%)
    pallas_call x1, Pallas kernels, shards(): results = call(*args)  46.3 us
    pallas_call x1, Pallas kernels, shards(): pl.pallas_call(store, out_shape=(jax.ShapeDtypeStruct((ITERS,), F32), jax...  1.41 us

profile of v8, /device:TPU:1, one launch (start us, length us, event | category | flops | bytes accessed | tf_op | source)
XLA Modules:
  0.0 48.4 jit_solution(1691958516703111696)
XLA Ops:
  0.6 46.3 %ascent.1 = (f32[8,128]{1,0:T(8,128)S(1)}, f32[3,16,2048]{2,1,0:T(8,128)S(1)}, f32[3,16,2048]{2,1,0:T(8,128)S(1)}) custom-call(f32[16,2048]{1,0:T(8,128)} %refs_0_.1, bf16[16,2048]{1,0:T(8,128)(2,1)} %refs_1_.1, bf16[16,2048]{1,0:T(8,128)(2,1)} %refs_2_.1, bf16[3,16,2048]{2,1,0:T(8,128)(2,1)} %refs_3_.1, bf16[3,16,2048]{2,1,0:T(8,128)(2,1)} %refs_4_.1, ...), custom_call_target="tpu_custom_call" | custom-call | tf_op jit(solution)/shard_map/ascent/pallas_call | solution.py:669
  46.9 1.4 %store.1 = (f32[3]{0:T(128)}, f32[3,16,2048]{2,1,0:T(8,128)}, f32[3,16,2048]{2,1,0:T(8,128)}) custom-call(f32[8,128]{1,0:T(8,128)S(1)} %get-tuple-element.6.bounds_v, f32[3,16,2048]{2,1,0:T(8,128)S(1)} %get-tuple-element.7.lam_v, f32[3,16,2048]{2,1,0:T(8,128)S(1)} %get-tuple-element.8.mu_v), custom_call_target="tpu_custom_call" | custom-call | tf_op jit(solution)/shard_map/store/pallas_call | solution.py:670
